TPU v7x, 256 devices: a whole 4x4x8 slice. The times are simulated.
256 devices in a mesh: span: 8 (over x, y_hi), stream: 32 (over z, y_lo, core).
Axes of the slice: x: 4, y: 4 (y_hi: 2, y_lo: 2; y = y_hi * 2 + y_lo), z: 8, core: 2. Of those that a mesh axis runs over, the one named last changes fastest.
Arguments:
- state: float32 [6, 64, 131072], P(None, None, ('span', 'stream')), may hold values from -6 to 6
- stiffness: float32 [131072], P(('span', 'stream')), may hold values from 0.3 to 6
- crossing: int32 [2, 32768], P(None, ('span', 'stream')), may hold values from 0 to 511, as said below
- contact_send: int32 [2, 8, 262144], P(None, None, ('span', 'stream')), may hold values from 0 to 32767
- contact_recv: int32 [2, 8, 262144], P(None, None, ('span', 'stream')), may hold values from 0 to 32767
- contact_fill: int32 [2, 8, 2048], P(None, None, ('span', 'stream')), may hold values from 0 to 128, as said below
Outputs:
- final_state: float32 [6, 64, 131072], P(None, None, ('span', 'stream'))
Inputs may be any that keep to these rules, and one draw needn't show every extreme that they name: `crossing`: each slab's 2 * 64 entries of one step are distinct and include slots 0 and 511. `contact_fill`: in each run of 8 blocks the live blocks come first; all full except the last live one; some runs have every block live.
All inputs are finite; a program needn't handle non-finite values.
Results may differ from a plain program's by a relative error of at most 0.0001.
Values sent between devices are 32-bit elements; how exact they have to be, the bound alone decides.
No kernel may reach another device: no remote copies, remote signals or barrier semaphores. Data moves between devices by JAX's collectives and lax.ppermute only.
A program may use at most 128 MiB of HBM per device.

v0:
```python
import functools

import jax
import jax.numpy as jnp
from jax import lax
from jax.experimental import pallas as pl
from jax.experimental.pallas import tpu as pltpu
from jax.sharding import PartitionSpec as P

STEPS = 2
BLOCK = 128
F32 = jnp.float32
BF16 = jnp.bfloat16
VMEM_LIMIT = 48 * 1024 * 1024


def split2(x):
    hi = x.astype(BF16)
    lo = (x - hi.astype(F32)).astype(BF16)
    return hi, lo


def split3(x):
    hi = x.astype(BF16)
    rest = x - hi.astype(F32)
    mid = rest.astype(BF16)
    lo = (rest - mid.astype(F32)).astype(BF16)
    return hi, mid, lo


def hot(index, count):
    rows = lax.broadcasted_iota(jnp.int32, (count, index.shape[1]), 0)
    return jnp.where(rows == index, 1.0, 0.0).astype(BF16)


def dot_nt(a, b):
    return lax.dot_general(a, b, (((1,), (1,)), ((), ())), preferred_element_type=F32)


def gather_row(table, index, nodes, fdev):
    slot = jnp.bitwise_and(index, fdev - 1)
    node = jnp.right_shift(index, fdev.bit_length() - 1)
    got = jnp.dot(table, hot(slot, fdev), preferred_element_type=F32)
    half = 3 * nodes
    got = got[:half] + got[half:]
    mask = lax.broadcasted_iota(jnp.int32, (nodes, index.shape[1]), 0) == node
    return [
        jnp.sum(jnp.where(mask, got[c * nodes : (c + 1) * nodes], 0.0), axis=0, keepdims=True)
        for c in range(3)
    ]


def store_table(table_ref, positions):
    hi, lo = split2(positions)
    half = positions.shape[0]
    table_ref[:half] = hi
    table_ref[half:] = lo


def send_gather(table_ref, index_ref, fill_ref, out_ref, nodes, fdev):
    groups, quota = index_ref.shape
    lane = lax.broadcasted_iota(jnp.int32, (1, BLOCK), 1)

    @pl.loop(0, groups)
    def _(g):
        rows = gather_row(table_ref[...], index_ref[pl.ds(g, 1), :], nodes, fdev)
        for c in range(3):
            out_ref[g, pl.ds(c, 1), :] = rows[c]
        for b in range(quota // BLOCK):
            live = jnp.where(lane < fill_ref[g, b], 1.0, 0.0)
            out_ref[g, pl.ds(3, 1), pl.ds(b * BLOCK, BLOCK)] = live


def fold(values, rows_ref):
    rows = values.shape[0]
    for i in range(values.shape[1] // BLOCK):
        rows_ref[i * rows : (i + 1) * rows] = values[:, i * BLOCK : (i + 1) * BLOCK]


def unfold(rows_ref, rows):
    chunks = rows_ref.shape[0] // rows
    return jnp.concatenate([rows_ref[i * rows : (i + 1) * rows] for i in range(chunks)], axis=1)


def fold_coef(coef, fields):
    chunks = coef.shape[1] // BLOCK
    return jnp.concatenate(
        [jnp.broadcast_to(coef[:, i * BLOCK : (i + 1) * BLOCK], (fields, BLOCK)) for i in range(chunks)], axis=0
    )


def factor(coef, inv_ref, elim_ref):
    inv = 1.0 / (1.0 + coef)
    for k in range(inv_ref.shape[0]):
        if k:
            inv = 1.0 / (1.0 + 2.0 * coef - coef * elim)
        elim = coef * inv
        inv_ref[k] = inv
        elim_ref[k] = elim


def solve(rows_ref, coef, inv_ref, elim_ref, nodes):
    half = nodes // 2
    lines = coef.shape[0]

    def at(n):
        return rows_ref[pl.ds(n, lines, stride=nodes), :]

    def put(n, value):
        rows_ref[pl.ds(n, lines, stride=nodes), :] = value

    top = at(0) * inv_ref[0]
    bot = at(nodes - 1) * inv_ref[0]
    tops, bots = [top], [bot]
    for k in range(1, half - 1):
        inv = inv_ref[k]
        elim = elim_ref[k]
        top = at(k) * inv + elim * top
        bot = at(nodes - 1 - k) * inv + elim * bot
        tops.append(top)
        bots.append(bot)
    left = at(half - 1) + coef * top
    right = at(half) + coef * bot
    pivot = 1.0 + 2.0 * coef - coef * elim_ref[half - 2]
    even = (left + right) * (0.5 / (pivot - coef))
    odd = (left - right) * (0.5 / (pivot + coef))
    top, bot = even + odd, even - odd
    put(half - 1, top)
    put(half, bot)
    for k in range(half - 2, -1, -1):
        elim = elim_ref[k]
        top = tops[k] + elim * top
        bot = bots[k] + elim * bot
        put(k, top)
        put(nodes - 1 - k, bot)


def pick(values, cross_hot):
    rows = values.shape[0]
    got = jnp.dot(jnp.concatenate(split3(values), axis=0), cross_hot, preferred_element_type=F32)
    return (got[:rows] + got[rows : 2 * rows]) + got[2 * rows :]


def place(values, cross_hot):
    rows = values.shape[0]
    got = dot_nt(jnp.concatenate(split3(values), axis=0), cross_hot)
    return (got[:rows] + got[rows : 2 * rows]) + got[2 * rows :]


def pack(leavers):
    rows = leavers.shape[0] // 2
    half = leavers.shape[1] // 2
    first, second = leavers[:rows], leavers[rows:]
    low = lax.broadcasted_iota(jnp.int32, first.shape, 1) < half
    up = jnp.where(low, first, pltpu.roll(second, half, 1))
    down = jnp.where(low, pltpu.roll(first, half, 1), second)
    return up, down


def unpack(up, down):
    half = up.shape[1] // 2
    low = lax.broadcasted_iota(jnp.int32, up.shape, 1) < half
    first = jnp.where(low, up, pltpu.roll(down, half, 1))
    second = jnp.where(low, pltpu.roll(up, half, 1), down)
    return first, second


def first_kernel(state_ref, index_ref, fill_ref, out_ref, table_ref, *, nodes, fdev):
    store_table(table_ref, state_ref[: 3 * nodes])
    send_gather(table_ref, index_ref, fill_ref, out_ref, nodes, fdev)


def local_kernel(
    state_ref, coef_ref, cross_ref, index_ref,
    local_ref, inv_ref, elim_ref, rot_ref, up_ref, down_ref,
    table_ref, rows_ref, *, nodes, fdev,
):
    half_rows = 3 * nodes
    groups = index_ref.shape[0]
    store_table(table_ref, state_ref[:half_rows])

    @pl.loop(0, groups)
    def _(g):
        rows = gather_row(table_ref[...], index_ref[pl.ds(g, 1), :], nodes, fdev)
        for c in range(3):
            local_ref[g, pl.ds(c, 1), :] = rows[c]

    coef = coef_ref[...]
    folded = fold_coef(coef, 3)
    factor(folded, inv_ref, elim_ref)
    fold(state_ref[half_rows:], rows_ref)
    solve(rows_ref, folded, inv_ref, elim_ref, nodes)
    rot_ref[...] = unfold(rows_ref, half_rows)
    cross_hot = hot(cross_ref[...], fdev)
    up, down = pack(pick(rot_ref[...], cross_hot))
    rows = up.shape[0]
    up_ref[:rows] = up
    down_ref[:rows] = down
    moved = pick(jnp.broadcast_to(coef, (8, fdev)), cross_hot)
    up_ref[rows:] = moved
    down_ref[rows:] = pltpu.roll(moved, moved.shape[1] // 2, 1)


def contact_kernel(
    got_ref, local_ref, index_ref, state_ref, coef_ref, inv_ref, elim_ref, cross_ref, rup_ref, rdown_ref,
    pos_ref, up_ref, down_ref,
    acc_ref, rows_ref, *, nodes, fdev,
):
    half_rows = 3 * nodes
    groups = index_ref.shape[0]
    acc_ref[...] = jnp.zeros_like(acc_ref)

    @pl.loop(0, groups)
    def _(g):
        index = index_ref[pl.ds(g, 1), :]
        slot = jnp.bitwise_and(index, fdev - 1)
        node = jnp.right_shift(index, fdev.bit_length() - 1)
        delta = [got_ref[g, pl.ds(c, 1), :] - local_ref[g, pl.ds(c, 1), :] for c in range(3)]
        radius = delta[0] * delta[0] + delta[1] * delta[1] + delta[2] * delta[2]
        scale = jnp.where(got_ref[g, pl.ds(3, 1), :] > 0.5, 1.0 / (1.0 + radius), 0.0)
        mask = lax.broadcasted_iota(jnp.int32, (nodes, index.shape[1]), 0) == node
        highs, lows = [], []
        for c in range(3):
            hi, lo = split2(delta[c] * scale)
            highs.append(jnp.where(mask, hi.astype(F32), 0.0).astype(BF16))
            lows.append(jnp.where(mask, lo.astype(F32), 0.0).astype(BF16))
        spread = jnp.concatenate(highs + lows, axis=0)
        acc_ref[...] += dot_nt(spread, hot(slot, fdev))

    fold(state_ref[:half_rows] + 0.5 * (acc_ref[:half_rows] + acc_ref[half_rows:]), rows_ref)
    solve(rows_ref, fold_coef(coef_ref[...], 3), inv_ref, elim_ref, nodes)
    pos_ref[...] = unfold(rows_ref, half_rows)
    up, down = pack(pick(pos_ref[...], hot(cross_ref[...], fdev)))
    rows = up.shape[0]
    up_ref[:rows] = up
    down_ref[:rows] = down
    up_ref[rows:] = rup_ref[...]
    down_ref[rows:] = rdown_ref[...]


def arrive(up_ref, down_ref, pos_ref, rot_ref, cross_ref, out_ref, nodes, fdev):
    part = 3 * nodes // 2
    cross_hot = hot(cross_ref[...], fdev)
    ones = jnp.ones((8, cross_hot.shape[1]), BF16)
    keep = dot_nt(ones, cross_hot)[0:1] < 0.5
    for side, ref in ((0, pos_ref), (1, rot_ref)):
        rows = pl.ds(side * part, part)
        first, second = unpack(up_ref[rows, :], down_ref[rows, :])
        placed = place(jnp.concatenate([first, second], axis=0), cross_hot)
        out_ref[pl.ds(side * 2 * part, 2 * part), :] = jnp.where(keep, ref[...], placed)
    return cross_hot, keep


def next_kernel(
    up_ref, down_ref, pos_ref, rot_ref, coef_ref, cross_ref, index_ref, fill_ref,
    state_ref, coef_out_ref, out_ref,
    table_ref, *, nodes, fdev,
):
    cross_hot, keep = arrive(up_ref, down_ref, pos_ref, rot_ref, cross_ref, state_ref, nodes, fdev)
    rows = pl.ds(3 * nodes, 8)
    first, _ = unpack(up_ref[rows, :], down_ref[rows, :])
    coef_out_ref[...] = jnp.where(keep, coef_ref[...], place(first, cross_hot)[0:1])
    store_table(table_ref, state_ref[: 3 * nodes])
    send_gather(table_ref, index_ref, fill_ref, out_ref, nodes, fdev)


def last_kernel(up_ref, down_ref, pos_ref, rot_ref, cross_ref, state_ref, *, nodes, fdev):
    arrive(up_ref, down_ref, pos_ref, rot_ref, cross_ref, state_ref, nodes, fdev)


def shifted(block, axis, distance):
    devices = range(lax.axis_size(axis))
    route = [((i - distance) % len(devices), i) for i in devices]
    return lax.ppermute(block, axis, route)


def per_device(state, stiffness, crossing, contact_send, contact_recv, contact_fill):
    fields, nodes, fdev = state.shape
    _, groups, quota = contact_send.shape
    cross = crossing.shape[1]
    rows = 3 * nodes
    moved = rows + 8
    vmem = pl.BlockSpec(memory_space=pltpu.VMEM)
    smem = pl.BlockSpec(memory_space=pltpu.SMEM)
    sent_shape = jax.ShapeDtypeStruct((groups, 4, quota), F32)
    table = pltpu.VMEM((2 * rows, fdev), BF16)

    def sds(*shape):
        return jax.ShapeDtypeStruct(shape, F32)

    lines = 3 * fdev // BLOCK
    factors = sds(nodes // 2, lines, BLOCK)
    folded = pltpu.VMEM((lines * nodes, BLOCK), F32)

    def call(kernel, name, ins, outs, scratch, flops):
        return pl.pallas_call(
            functools.partial(kernel, nodes=nodes, fdev=fdev),
            out_shape=outs,
            in_specs=ins,
            out_specs=[vmem] * len(outs),
            scratch_shapes=scratch,
            name=name,
            cost_estimate=pl.CostEstimate(flops=flops, bytes_accessed=4 * fields * nodes * fdev, transcendentals=0),
            compiler_params=pltpu.CompilerParams(vmem_limit_bytes=VMEM_LIMIT),
        )

    matmul = 2 * 2 * rows * fdev * groups * quota
    xcur = state.reshape(fields * nodes, fdev)
    coef = stiffness.reshape(1, fdev)
    (sent,) = call(first_kernel, "send_first", [vmem, vmem, smem], [sent_shape], [table], matmul)(
        xcur, contact_send[0], contact_fill[0]
    )
    for step in range(STEPS):
        got = lax.all_to_all(sent, "span", split_axis=0, concat_axis=0, tiled=True)
        crossing_now = crossing[step].reshape(1, cross)
        local, inv, elim, rot, rup, rdown = call(
            local_kernel, "local", [vmem] * 4,
            [sds(groups, 3, quota), factors, factors, sds(rows, fdev),
             sds(rows // 2 + 8, cross), sds(rows // 2 + 8, cross)],
            [table, folded], matmul,
        )(xcur, coef, crossing_now, contact_recv[step])
        pos, up, down = call(
            contact_kernel, "contact", [vmem] * 10,
            [sds(rows, fdev), sds(moved, cross), sds(moved, cross)],
            [pltpu.VMEM((2 * rows, fdev), F32), folded], matmul,
        )(got, local, contact_recv[step], xcur, coef, inv, elim, crossing_now, rup, rdown)
        up = shifted(up, "stream", 1)
        down = shifted(down, "stream", -1)
        if step + 1 < STEPS:
            xcur, coef, sent = call(
                next_kernel, "send_next", [vmem] * 7 + [smem],
                [sds(fields * nodes, fdev), sds(1, fdev), sent_shape], [table], matmul,
            )(up, down, pos, rot, coef, crossing_now, contact_send[step + 1], contact_fill[step + 1])
        else:
            (xcur,) = call(last_kernel, "arrive", [vmem] * 5, [sds(fields * nodes, fdev)], [], matmul // 8)(
                up, down, pos, rot, crossing_now
            )
    return xcur.reshape(fields, nodes, fdev)


def solution(mesh):
    placed = (
        P(None, None, ("span", "stream")),
        P(("span", "stream")),
        P(None, ("span", "stream")),
        P(None, None, ("span", "stream")),
        P(None, None, ("span", "stream")),
        P(None, None, ("span", "stream")),
    )
    return jax.shard_map(
        per_device,
        mesh=mesh,
        in_specs=placed,
        out_specs=P(None, None, ("span", "stream")),
        check_vma=False,
    )
```

profile of v0, /device:TPU:105, one launch (start us, length us, event | category | flops | bytes accessed | tf_op | source)
XLA Modules:
  0.0 73.5 jit_solution(8330265231706281462)
XLA Ops:
  0.0 0.7 slice_bitcast_fusion.4
  0.7 0.8 %slice_bitcast_fusion.1 = (s32[8,1024]{1,0:T(8,128)S(1)}, s32[8,1024]{1,0:T(8,128)S(1)}) fusion(s32[2,8,1024]{2,1,0:T(8,128)} %param.9), kind=kLoop, calls=%fused_computation.1 | loop fusion | bytes 131072 | tf_op jit(solution)/shard_map/squeeze | solution.py:333
  1.5 0.0 copy-start
  1.5 1.1 %copy-done = f32[6,64,512]{2,1,0:T(8,128)S(1)} copy-done((f32[6,64,512]{2,1,0:T(8,128)S(1)}, f32[6,64,512]{2,1,0:T(8,128)}, u32[]{:S(2)}) %copy-start) | copy-done | bytes 786456
  2.6 0.0 copy-start.1
  2.6 6.1 %send_first.1 = f32[8,4,1024]{2,1,0:T(4,128)} custom-call(f32[384,512]{1,0:T(8,128)S(1)} %bitcast.15, s32[8,1024]{1,0:T(8,128)S(1)} %get-tuple-element.50.index_ref, s32[8,8]{1,0:T(8,128)S(1)} %get-tuple-element.52.fill_ref), custom_call_target="tpu_custom_call" | custom-call | flops 3221225472 | bytes 786432 | tf_op jit(solution)/shard_map/send_first/pallas_call | solution.py:310
  8.7 0.0 copy-start.4
  8.7 0.0 copy-start.3
  8.7 5.9 %all-to-all-start = ((f32[8,4,1024]{2,1,0:T(4,128)}), f32[8,4,1024]{2,1,0:T(4,128)S(1)}, u32[]{:S(2)}, u32[]{:S(2)}) async-start(f32[8,4,1024]{2,1,0:T(4,128)} %send_first.1), calls=%async_computation | async-start | bytes 262144 | tf_op jit(solution)/shard_map/all_to_all | solution.py:314
  14.6 0.0 copy-done.4
  14.6 0.0 copy-done.3
  14.6 0.0 copy-start.2
  14.6 0.0 copy-done.1
  14.7 0.7 copy-done.2
  15.3 5.9 %local.2 = (f32[8,3,1024]{2,1,0:T(4,128)S(1)}, f32[32,12,128]{2,1,0:T(8,128)S(1)}, f32[32,12,128]{2,1,0:T(8,128)S(1)}, f32[192,512]{1,0:T(8,128)S(1)}, f32[104,128]{1,0:T(8,128)S(1)}, /*index=5*/f32[104,128]{1,0:T(8,128)S(1)}) custom-call(f32[384,512]{1,0:T(8,128)S(1)} %bitcast.16, f32[1,512]{1,0:T(1,128)S(1)} %bitcast.18, ...), custom_call_target="tpu_custom_call" | custom-call | flops 3221225472 | bytes 786432 | tf_op jit(solution)/shard_map/local/pallas_call | solution.py:316
  21.3 0.1 all-to-all-done.got_ref
  21.3 6.0 %contact.2 = (f32[192,512]{1,0:T(8,128)S(1)}, f32[200,128]{1,0:T(8,128)S(1)}, f32[200,128]{1,0:T(8,128)S(1)}) custom-call(f32[8,4,1024]{2,1,0:T(4,128)S(1)} %all-to-all-done.got_ref, f32[8,3,1024]{2,1,0:T(4,128)S(1)} %get-tuple-element.26.local_ref, s32[8,1024]{1,0:T(8,128)S(1)} %get-tuple-element.48.index_ref, f32[384,512]{1,0:T(8,128)S(1)} %bitcast.17, ...), custom_call_target="tpu_custom_call" | custom-call | flops 3221225472 | bytes 786432 | tf_op jit(solution)/shard_map/contact/pallas_call | solution.py:322
  27.4 5.7 %collective-permute-start = (f32[200,128]{1,0:T(8,128)S(1)}, f32[200,128]{1,0:T(8,128)S(1)}, u32[]{:S(2)}, u32[]{:S(2)}) collective-permute-start(f32[200,128]{1,0:T(8,128)S(1)} %get-tuple-element.31), channel_id=1, source_target_pairs={{31,0},{0,1},{1,2},{2,3},{3,4},{4,5},{5,6},{6,7},{7,8},{8,9},{9,10... | collective-permute-start | bytes 307208 | tf_op jit(solution)/shard_map/ppermute | solution.py:274
  33.1 0.0 collective-permute-start.1
  33.1 1.7 %collective-permute-done.up_ref = f32[200,128]{1,0:T(8,128)S(1)} collective-permute-done((f32[200,128]{1,0:T(8,128)S(1)}, f32[200,128]{1,0:T(8,128)S(1)}, u32[]{:S(2)}, u32[]{:S(2)}) %collective-permute-start) | collective-permute-done | bytes 102432 | tf_op jit(solution)/shard_map/ppermute | solution.py:274
  34.8 4.5 %collective-permute-done.1.down_ref = f32[200,128]{1,0:T(8,128)S(1)} collective-permute-done((f32[200,128]{1,0:T(8,128)S(1)}, f32[200,128]{1,0:T(8,128)S(1)}, u32[]{:S(2)}, u32[]{:S(2)}) %collective-permute-start.1) | collective-permute-done | bytes 102432 | tf_op jit(solution)/shard_map/ppermute | solution.py:274
  39.3 6.5 %send_next.1 = (f32[384,512]{1,0:T(8,128)S(1)}, f32[1,512]{1,0:T(1,128)S(1)}, f32[8,4,1024]{2,1,0:T(4,128)}) custom-call(f32[200,128]{1,0:T(8,128)S(1)} %collective-permute-done.up_ref, f32[200,128]{1,0:T(8,128)S(1)} %collective-permute-done.1.down_ref, f32[192,512]{1,0:T(8,128)S(1)} %get-tuple-element.33.pos_ref, f32[192,512]{1,0:T(8,128)S(1)} %get-tuple-element.34.rot_ref, ...), custom_call_target="tpu_custom_call" | custom-call | flops 3221225472 | bytes 786432 | tf_op jit(solution)/shard_map/send_next/pallas_call | solution.py:330
  45.8 5.1 %all-to-all-start.1 = ((f32[8,4,1024]{2,1,0:T(4,128)}), f32[8,4,1024]{2,1,0:T(4,128)S(1)}, u32[]{:S(2)}, u32[]{:S(2)}) async-start(f32[8,4,1024]{2,1,0:T(4,128)} %get-tuple-element.35), calls=%async_computation.1 | async-start | bytes 262144 | tf_op jit(solution)/shard_map/all_to_all | solution.py:314
  50.9 5.9 %local.3 = (f32[8,3,1024]{2,1,0:T(4,128)S(1)}, f32[32,12,128]{2,1,0:T(8,128)S(1)}, f32[32,12,128]{2,1,0:T(8,128)S(1)}, f32[192,512]{1,0:T(8,128)S(1)}, f32[104,128]{1,0:T(8,128)S(1)}, /*index=5*/f32[104,128]{1,0:T(8,128)S(1)}) custom-call(f32[384,512]{1,0:T(8,128)S(1)} %get-tuple-element.36.state_ref, f32[1,512]{1,0:T(1,128)S(1)} %get-tuple-element.37.coef_ref, ...), custom_call_target="tpu_custom_call" | custom-call | flops 3221225472 | bytes 786432 | tf_op jit(solution)/shard_map/local/pallas_call | solution.py:316
  56.8 0.8 %all-to-all-done.1.got_ref = f32[8,4,1024]{2,1,0:T(4,128)S(1)} async-done(((f32[8,4,1024]{2,1,0:T(4,128)}), f32[8,4,1024]{2,1,0:T(4,128)S(1)}, u32[]{:S(2)}, u32[]{:S(2)}) %all-to-all-start.1) | async-done | bytes 131104 | tf_op jit(solution)/shard_map/all_to_all | solution.py:314
  57.7 6.0 %contact.3 = (f32[192,512]{1,0:T(8,128)S(1)}, f32[200,128]{1,0:T(8,128)S(1)}, f32[200,128]{1,0:T(8,128)S(1)}) custom-call(f32[8,4,1024]{2,1,0:T(4,128)S(1)} %all-to-all-done.1.got_ref, f32[8,3,1024]{2,1,0:T(4,128)S(1)} %get-tuple-element.38.local_ref, s32[8,1024]{1,0:T(8,128)S(1)} %get-tuple-element.47.index_ref, ...), custom_call_target="tpu_custom_call" | custom-call | flops 3221225472 | bytes 786432 | tf_op jit(solution)/shard_map/contact/pallas_call | solution.py:322
  63.7 2.2 %collective-permute-start.2 = (f32[200,128]{1,0:T(8,128)S(1)}, f32[200,128]{1,0:T(8,128)S(1)}, u32[]{:S(2)}, u32[]{:S(2)}) collective-permute-start(f32[200,128]{1,0:T(8,128)S(1)} %get-tuple-element.43), channel_id=1, source_target_pairs={{31,0},{0,1},{1,2},{2,3},{3,4},{4,5},{5,6},{6,7},{7,8},{8,9},{9,10... | collective-permute-start | bytes 307208 | tf_op jit(solution)/shard_map/ppermute | solution.py:274
  65.9 0.0 collective-permute-start.3
  65.9 1.7 %collective-permute-done.2.up_ref = f32[200,128]{1,0:T(8,128)S(1)} collective-permute-done((f32[200,128]{1,0:T(8,128)S(1)}, f32[200,128]{1,0:T(8,128)S(1)}, u32[]{:S(2)}, u32[]{:S(2)}) %collective-permute-start.2) | collective-permute-done | bytes 102432 | tf_op jit(solution)/shard_map/ppermute | solution.py:274
  67.6 4.5 %collective-permute-done.3.down_ref = f32[200,128]{1,0:T(8,128)S(1)} collective-permute-done((f32[200,128]{1,0:T(8,128)S(1)}, f32[200,128]{1,0:T(8,128)S(1)}, u32[]{:S(2)}, u32[]{:S(2)}) %collective-permute-start.3) | collective-permute-done | bytes 102432 | tf_op jit(solution)/shard_map/ppermute | solution.py:274
  72.1 1.4 %arrive.1 = f32[384,512]{1,0:T(8,128)} custom-call(f32[200,128]{1,0:T(8,128)S(1)} %collective-permute-done.2.up_ref, f32[200,128]{1,0:T(8,128)S(1)} %collective-permute-done.3.down_ref, f32[192,512]{1,0:T(8,128)S(1)} %get-tuple-element.45.pos_ref, f32[192,512]{1,0:T(8,128)S(1)} %get-tuple-element.46.rot_ref, s32[1,128]{1,0:T(1,128)S(1)} %get-tuple-element.53.cross_ref), custom_call_target="tpu_custom_call" | custom-call | flops 402653184 | bytes 786432 | tf_op jit(solution)/shard_map/arrive/pallas_call | solution.py:335
  (2 shorter events, 0.0 us)
Async XLA Ops:
  1.5 1.1 %copy-start = (f32[6,64,512]{2,1,0:T(8,128)S(1)}, f32[6,64,512]{2,1,0:T(8,128)}, u32[]{:S(2)}) copy-start(f32[6,64,512]{2,1,0:T(8,128)} %param.6) | copy-start | bytes 2359300
  2.6 12.0 %copy-start.1 = (f32[6,64,512]{2,1,0:T(8,128)S(1)}, f32[6,64,512]{2,1,0:T(8,128)}, u32[]{:S(2)}) copy-start(f32[6,64,512]{2,1,0:T(8,128)} %param.6) | copy-start | bytes 2359300
  8.7 5.9 %copy-start.4 = (s32[2,128]{1,0:T(2,128)S(1)}, s32[2,128]{1,0:T(2,128)}, u32[]{:S(2)}) copy-start(s32[2,128]{1,0:T(2,128)} %param.8) | copy-start | bytes 3076
  8.7 5.9 %copy-start.3 = (s32[2,8,1024]{2,1,0:T(8,128)S(1)}, s32[2,8,1024]{2,1,0:T(8,128)}, u32[]{:S(2)}) copy-start(s32[2,8,1024]{2,1,0:T(8,128)} %param.10) | copy-start | bytes 196612
  8.7 12.6 %all-to-all-start = ((f32[8,4,1024]{2,1,0:T(4,128)}), f32[8,4,1024]{2,1,0:T(4,128)S(1)}, u32[]{:S(2)}, u32[]{:S(2)}) async-start(f32[8,4,1024]{2,1,0:T(4,128)} %send_first.1), calls=%async_computation | async-start | bytes 262144 | tf_op jit(solution)/shard_map/all_to_all | solution.py:314
  14.6 0.7 copy-start.2
  27.4 7.4 %collective-permute-start = (f32[200,128]{1,0:T(8,128)S(1)}, f32[200,128]{1,0:T(8,128)S(1)}, u32[]{:S(2)}, u32[]{:S(2)}) collective-permute-start(f32[200,128]{1,0:T(8,128)S(1)} %get-tuple-element.31), channel_id=1, source_target_pairs={{31,0},{0,1},{1,2},{2,3},{3,4},{4,5},{5,6},{6,7},{7,8},{8,9},{9,10... | collective-permute-start | bytes 307208 | tf_op jit(solution)/shard_map/ppermute | solution.py:274
  33.1 6.2 %collective-permute-start.1 = (f32[200,128]{1,0:T(8,128)S(1)}, f32[200,128]{1,0:T(8,128)S(1)}, u32[]{:S(2)}, u32[]{:S(2)}) collective-permute-start(f32[200,128]{1,0:T(8,128)S(1)} %get-tuple-element.32), channel_id=1, source_target_pairs={{1,0},{2,1},{3,2},{4,3},{5,4},{6,5},{7,6},{8,7},{9,8},{10,9},{11,1... | collective-permute-start | bytes 307208 | tf_op jit(solution)/shard_map/ppermute | solution.py:274
  45.8 11.8 %all-to-all-start.1 = ((f32[8,4,1024]{2,1,0:T(4,128)}), f32[8,4,1024]{2,1,0:T(4,128)S(1)}, u32[]{:S(2)}, u32[]{:S(2)}) async-start(f32[8,4,1024]{2,1,0:T(4,128)} %get-tuple-element.35), calls=%async_computation.1 | async-start | bytes 262144 | tf_op jit(solution)/shard_map/all_to_all | solution.py:314
  63.7 3.9 %collective-permute-start.2 = (f32[200,128]{1,0:T(8,128)S(1)}, f32[200,128]{1,0:T(8,128)S(1)}, u32[]{:S(2)}, u32[]{:S(2)}) collective-permute-start(f32[200,128]{1,0:T(8,128)S(1)} %get-tuple-element.43), channel_id=1, source_target_pairs={{31,0},{0,1},{1,2},{2,3},{3,4},{4,5},{5,6},{6,7},{7,8},{8,9},{9,10... | collective-permute-start | bytes 307208 | tf_op jit(solution)/shard_map/ppermute | solution.py:274
  65.9 6.2 %collective-permute-start.3 = (f32[200,128]{1,0:T(8,128)S(1)}, f32[200,128]{1,0:T(8,128)S(1)}, u32[]{:S(2)}, u32[]{:S(2)}) collective-permute-start(f32[200,128]{1,0:T(8,128)S(1)} %get-tuple-element.44), channel_id=1, source_target_pairs={{1,0},{2,1},{3,2},{4,3},{5,4},{6,5},{7,6},{8,7},{9,8},{10,9},{11,1... | collective-permute-start | bytes 307208 | tf_op jit(solution)/shard_map/ppermute | solution.py:274
where the time goes:
time: 74 us; the launch traced here: 73.5 us
  Pallas kernels  37.9 us (51%)
  starting transfers between devices  18.9 us (26%)
  waiting for transfers between devices  13.3 us (18%)
  local copies, waits for them, and re-layouts  3.31 us (4%)
    ppermute x4, waiting for transfers between devices, shifted(): return lax.ppermute(block, axis, route)  12.4 us
    pallas_call x2, Pallas kernels, per_device(): call(contact_kernel, 'contact', [vmem] * 10, [sds(rows, fdev), sds(moved,...  12 us
    pallas_call x2, Pallas kernels, per_device(): call(local_kernel, 'local', [vmem] * 4, [sds(groups, 3, quota), factors,...  11.9 us
    all_to_all x2, starting transfers between devices, per_device(): got = lax.all_to_all(sent, 'span', split_axis=0, concat_axis=0, tiled=True)  11 us
    ppermute x4, starting transfers between devices, shifted(): return lax.ppermute(block, axis, route)  7.94 us
    pallas_call x1, Pallas kernels, per_device(): call(next_kernel, 'send_next', [vmem] * 7 + [smem], [sds(fields * nodes,...  6.54 us
    pallas_call x1, Pallas kernels, per_device(): call(first_kernel, 'send_first', [vmem, vmem, smem], [sent_shape], [table...  6.08 us
    unnamed x10, local copies, waits for them, and re-layouts  1.81 us
  transfers between devices with their start and end apart: 6, of which 6 were waited for; matrix products, arithmetic and copies ran while one was open for 0% of the time, Pallas kernels for 16%

commit v1 on v0

v1 whole, which is shorter than its diff:
```python
import functools

import jax
import jax.numpy as jnp
from jax import lax
from jax.experimental import pallas as pl
from jax.experimental.pallas import tpu as pltpu
from jax.sharding import PartitionSpec as P

STEPS = 2
BLOCK = 128
LANES = 256
CHUNK = 8
F32 = jnp.float32
BF16 = jnp.bfloat16
VMEM_LIMIT = 48 * 1024 * 1024
FIRST_LIMIT = 63 * 1024 * 1024


def split2(x):
    hi = x.astype(BF16)
    lo = (x - hi.astype(F32)).astype(BF16)
    return hi, lo


def split3(x):
    hi = x.astype(BF16)
    rest = x - hi.astype(F32)
    mid = rest.astype(BF16)
    lo = (rest - mid.astype(F32)).astype(BF16)
    return hi, mid, lo


def hot(index, count):
    rows = lax.broadcasted_iota(jnp.int32, (count, index.shape[1]), 0)
    return jnp.where(rows == index, 1.0, 0.0).astype(BF16)


def dot_nt(a, b):
    return lax.dot_general(a, b, (((1,), (1,)), ((), ())), preferred_element_type=F32)


def parts_of(index, nodes):
    per_node = index >> (LANES.bit_length() - 1)
    lane = index & (LANES - 1)
    return lane, per_node


def row_key(per_node, nodes, fdev):
    wide = fdev // LANES
    return (per_node & (wide - 1)) * nodes + (per_node >> (wide.bit_length() - 1))


def store_table(table_ref, positions, nodes):
    wide = positions.shape[1] // LANES
    rows = 3 * wide * nodes
    for c in range(3):
        for w in range(wide):
            hi, lo = split2(positions[c * nodes : (c + 1) * nodes, w * LANES : (w + 1) * LANES])
            at = (c * wide + w) * nodes
            table_ref[at : at + nodes] = hi
            table_ref[rows + at : rows + at + nodes] = lo


def gather_row(table, index, nodes, fdev, between=lambda: None):
    lane, per_node = parts_of(index, nodes)
    key = row_key(per_node, nodes, fdev)
    got = jnp.dot(table, hot(lane, LANES), preferred_element_type=F32)
    between()
    rows = got.shape[0] // 2
    keys = rows // 3
    relative = key - lax.broadcasted_iota(jnp.int32, (8, index.shape[1]), 0)
    out = []
    for c in range(3):
        acc = jnp.zeros((8, index.shape[1]), F32)
        for j in range(0, keys, 8):
            at = c * keys + j
            acc = jnp.where(relative == j, got[at : at + 8] + got[rows + at : rows + at + 8], acc)
        out.append(jnp.sum(acc, axis=0, keepdims=True))
    return out


def list_live(live_of, list_ref, groups, blocks):
    count = jnp.int32(0)
    for g in range(groups):
        for b in range(blocks):
            list_ref[count] = g * blocks + b
            count = count + live_of(g, b)
    return count


def index_chunk(index_ref, ids, groups, blocks):
    rows = [(n & (blocks - 1)) * groups + (n >> (blocks.bit_length() - 1)) for n in ids]
    return jnp.concatenate([index_ref[pl.ds(n, 1), :] for n in rows], axis=1)


def put_chunk(out_ref, ids, rows, blocks):
    for k, n in enumerate(ids):
        for c in range(3):
            at = c * blocks + (n & (blocks - 1))
            out_ref[n >> (blocks.bit_length() - 1), pl.ds(at, 1), :] = rows[c][:, k * BLOCK : (k + 1) * BLOCK]


def gather_live(table_ref, index_ref, out_ref, list_ref, count, groups, blocks, nodes, fdev):
    @pl.loop(0, (count + CHUNK - 1) // CHUNK)
    def _(i):
        ids = [list_ref[jnp.minimum(i * CHUNK + k, count - 1)] for k in range(CHUNK)]
        index = index_chunk(index_ref, ids, groups, blocks)
        put_chunk(out_ref, ids, gather_row(table_ref[...], index, nodes, fdev), blocks)


def send_gather(table_ref, index_ref, fill_ref, out_ref, list_ref, step, nodes, fdev):
    groups, lines, _ = out_ref.shape
    blocks = lines // 4
    low = lax.broadcasted_iota(jnp.int32, (1, BLOCK), 1) < BLOCK // 2
    out_ref[...] = jnp.zeros_like(out_ref)
    count = list_live(lambda g, b: (fill_ref[step, g, b] > 0).astype(jnp.int32), list_ref, groups, blocks)
    for g in range(groups):
        for b in range(blocks):
            fills = jnp.where(low, fill_ref[step, g, b], fill_ref[STEPS - 1, g, b])
            out_ref[g, pl.ds(3 * blocks + b, 1), :] = fills.astype(F32)
    gather_live(table_ref, index_ref, out_ref, list_ref, count, groups, blocks, nodes, fdev)


def live_words(got_ref, blocks, lane):
    sub = lax.broadcasted_iota(jnp.int32, (blocks, BLOCK), 0)
    here = lax.broadcasted_iota(jnp.int32, (blocks, BLOCK), 1) == lane
    words = []
    for g in range(got_ref.shape[0]):
        live = (got_ref[g, 3 * blocks :] > 0.5) & here
        words.append(jnp.sum(jnp.where(live, jnp.left_shift(1, sub), 0).astype(F32)).astype(jnp.int32))
    return words


def fold(values, rows_ref):
    rows = values.shape[0]
    for i in range(values.shape[1] // BLOCK):
        rows_ref[i * rows : (i + 1) * rows] = values[:, i * BLOCK : (i + 1) * BLOCK]


def unfold(rows_ref, rows):
    chunks = rows_ref.shape[0] // rows
    return jnp.concatenate([rows_ref[i * rows : (i + 1) * rows] for i in range(chunks)], axis=1)


def fold_coef(coef, fields):
    chunks = coef.shape[1] // BLOCK
    return jnp.concatenate(
        [jnp.broadcast_to(coef[:, i * BLOCK : (i + 1) * BLOCK], (fields, BLOCK)) for i in range(chunks)], axis=0
    )


def factor_steps(coef, inv_ref, elim_ref):
    inv = 1.0 / (1.0 + coef)
    for k in range(inv_ref.shape[0]):
        if k:
            inv = 1.0 / (1.0 + 2.0 * coef - coef * elim)
        elim = coef * inv
        inv_ref[k] = inv
        elim_ref[k] = elim
        yield


def solve_steps(get, put, hold_ref, coef, inv_ref, elim_ref, nodes):
    half = nodes // 2
    top = get(0) * inv_ref[0]
    bot = get(nodes - 1) * inv_ref[0]
    hold_ref[0] = top
    hold_ref[nodes - 1] = bot
    for k in range(1, half - 1):
        inv = inv_ref[k]
        elim = elim_ref[k]
        top = get(k) * inv + elim * top
        bot = get(nodes - 1 - k) * inv + elim * bot
        hold_ref[k] = top
        hold_ref[nodes - 1 - k] = bot
        yield
    left = get(half - 1) + coef * top
    right = get(half) + coef * bot
    pivot = 1.0 + 2.0 * coef - coef * elim_ref[half - 2]
    even = (left + right) * (0.5 / (pivot - coef))
    odd = (left - right) * (0.5 / (pivot + coef))
    top, bot = even + odd, even - odd
    put(half - 1, top)
    put(half, bot)
    yield
    for k in range(half - 2, -1, -1):
        elim = elim_ref[k]
        top = hold_ref[k] + elim * top
        bot = hold_ref[nodes - 1 - k] + elim * bot
        put(k, top)
        put(nodes - 1 - k, bot)
        yield


def strided(rows_ref, lines, nodes):
    def get(n):
        return rows_ref[pl.ds(n, lines, stride=nodes), :]

    def put(n, value):
        rows_ref[pl.ds(n, lines, stride=nodes), :] = value

    return get, put


def dense(hold_ref):
    def get(n):
        return hold_ref[n]

    def put(n, value):
        hold_ref[n] = value

    return get, put


def run(steps, count=None):
    done = 0
    while count is None or done < count:
        if next(steps, steps) is steps:
            return
        done += 1


def pick(values, cross_hot):
    rows = values.shape[0]
    got = jnp.dot(jnp.concatenate(split3(values), axis=0), cross_hot, preferred_element_type=F32)
    return (got[:rows] + got[rows : 2 * rows]) + got[2 * rows :]


def place(values, cross_hot):
    rows = values.shape[0]
    got = dot_nt(jnp.concatenate(split3(values), axis=0), cross_hot)
    return (got[:rows] + got[rows : 2 * rows]) + got[2 * rows :]


def pack(leavers):
    rows = leavers.shape[0] // 2
    half = leavers.shape[1] // 2
    first, second = leavers[:rows], leavers[rows:]
    low = lax.broadcasted_iota(jnp.int32, first.shape, 1) < half
    up = jnp.where(low, first, pltpu.roll(second, half, 1))
    down = jnp.where(low, pltpu.roll(first, half, 1), second)
    return up, down


def unpack(up, down):
    half = up.shape[1] // 2
    low = lax.broadcasted_iota(jnp.int32, up.shape, 1) < half
    first = jnp.where(low, up, pltpu.roll(down, half, 1))
    second = jnp.where(low, pltpu.roll(up, half, 1), down)
    return first, second


def first_kernel(
    state_ref, index_ref, fill_ref, out_ref, table_ref, list_ref, held_ref, index_held_ref, sems, *, nodes, fdev
):
    copy = pltpu.make_async_copy(state_ref.at[pl.ds(0, 3 * nodes)], held_ref, sems.at[0])
    index_copy = pltpu.make_async_copy(index_ref.at[0], index_held_ref, sems.at[1])
    copy.start()
    index_copy.start()
    index_copy.wait()
    copy.wait()
    store_table(table_ref, held_ref[...], nodes)
    send_gather(table_ref, index_held_ref, fill_ref, out_ref, list_ref, 0, nodes, fdev)


def local_kernel(
    state_ref, coef_ref, cross_ref, index_ref,
    local_ref, inv_ref, elim_ref, rot_ref, up_ref, down_ref,
    table_ref, rows_ref, hold_ref, *, nodes, fdev,
):
    half_rows = 3 * nodes
    groups, lines, _ = local_ref.shape
    blocks = lines // 3
    coef = coef_ref[...]
    folded = fold_coef(coef, 3)
    fold(state_ref[half_rows:], rows_ref)
    store_table(table_ref, state_ref[:half_rows], nodes)

    def chores():
        yield from factor_steps(folded, inv_ref, elim_ref)
        sparse, close = strided(rows_ref, folded.shape[0], nodes), dense(hold_ref)
        for step in range(STEPS):
            get = sparse[0] if step == 0 else close[0]
            put = sparse[1] if step == STEPS - 1 else close[1]
            yield from solve_steps(get, put, hold_ref, folded, inv_ref, elim_ref, nodes)

    steps = chores()
    chunks = groups * blocks // CHUNK
    share = -(-(nodes // 2 + STEPS * nodes) // chunks)
    for i in range(chunks):
        ids = [i * CHUNK + k for k in range(CHUNK)]
        index = index_chunk(index_ref.at[0], ids, groups, blocks)
        rows = gather_row(table_ref[...], index, nodes, fdev, lambda: run(steps, share))
        put_chunk(local_ref, ids, rows, blocks)
    run(steps)

    rot_ref[...] = unfold(rows_ref, half_rows)
    cross_hot = hot(cross_ref[pl.ds(0, 1), :], fdev)
    leave(rot_ref[...], coef, cross_hot, up_ref, down_ref)


def leave(rot, coef, cross_hot, up_ref, down_ref):
    up, down = pack(pick(rot, cross_hot))
    rows = up.shape[0]
    up_ref[:rows] = up
    down_ref[:rows] = down
    moved = pick(jnp.broadcast_to(coef, (8, coef.shape[1])), cross_hot)
    up_ref[rows:] = moved
    down_ref[rows:] = pltpu.roll(moved, moved.shape[1] // 2, 1)


def local_next_kernel(
    state_ref, up_ref, down_ref, rot_ref, coef_ref, cross_ref, index_ref, told_ref,
    local_ref, inv_ref, elim_ref, rot_out_ref, coef_out_ref, rup_ref, rdown_ref,
    table_ref, list_ref, *, step, nodes, fdev,
):
    groups, lines, _ = local_ref.shape
    blocks = lines // 3
    part = 3 * nodes // 2
    words = live_words(told_ref, blocks, BLOCK // 2)
    count = list_live(lambda g, b: (words[g] >> b) & 1, list_ref, groups, blocks)
    local_ref[...] = jnp.zeros_like(local_ref)
    cross_hot = hot(cross_ref[pl.ds(step - 1, 1), :], fdev)
    keep = kept(cross_hot)
    rows = pl.ds(3 * nodes, 8)
    first, _ = unpack(up_ref[rows, :], down_ref[rows, :])
    coef = jnp.where(keep, coef_ref[...], place(first, cross_hot)[0:1])
    coef_out_ref[...] = coef
    store_table(table_ref, state_ref[...], nodes)
    run(factor_steps(fold_coef(coef, 3), inv_ref, elim_ref))
    rot = arrive(up_ref, down_ref, rot_ref[...], cross_hot, keep, part)
    rot_out_ref[...] = rot
    leave(rot, coef, hot(cross_ref[pl.ds(step, 1), :], fdev), rup_ref, rdown_ref)
    gather_live(table_ref, index_ref.at[step], local_ref, list_ref, count, groups, blocks, nodes, fdev)


def contact_kernel(
    got_ref, local_ref, index_ref, state_ref, coef_ref, inv_ref, elim_ref, cross_ref, rup_ref, rdown_ref,
    pos_ref, up_ref, down_ref,
    acc_ref, rows_ref, hold_ref, force_ref, list_ref, *, step, nodes, fdev,
):
    half_rows = 3 * nodes
    groups, lines, _ = local_ref.shape
    blocks = lines // 3
    pairs = groups * blocks
    acc_ref[...] = jnp.zeros_like(acc_ref)
    force_ref[:, pairs:] = jnp.zeros_like(force_ref[:, pairs:])
    lanes = lax.broadcasted_iota(jnp.int32, (blocks, BLOCK), 1).astype(F32)
    words = live_words(got_ref, blocks, 0)
    for g in range(groups):
        delta = [
            got_ref[g, c * blocks : (c + 1) * blocks] - local_ref[g, c * blocks : (c + 1) * blocks] for c in range(3)
        ]
        radius = delta[0] * delta[0] + delta[1] * delta[1] + delta[2] * delta[2]
        live = lanes < got_ref[g, 3 * blocks :, 0:1]
        scale = 1.0 / (1.0 + radius)
        for c in range(3):
            force_ref[c, g * blocks : (g + 1) * blocks] = jnp.where(live, delta[c] * scale, 0.0)
    count = list_live(lambda g, b: (words[g] >> b) & 1, list_ref, groups, blocks)
    wide = fdev // LANES
    keys = wide * nodes

    @pl.loop(0, (count + CHUNK - 1) // CHUNK)
    def _(i):
        ids = [jnp.where(i * CHUNK + k < count, list_ref[i * CHUNK + k], pairs) for k in range(CHUNK)]
        index = index_chunk(index_ref.at[step], [jnp.minimum(n, pairs - 1) for n in ids], groups, blocks)
        lane, per_node = parts_of(index, nodes)
        key = row_key(per_node, nodes, fdev)
        mask = lax.broadcasted_iota(jnp.int32, (keys, index.shape[1]), 0) == key
        highs, lows = [], []
        for c in range(3):
            force = jnp.concatenate([force_ref[c, pl.ds(n, 1), :] for n in ids], axis=1)
            hi, lo = split2(force)
            highs.append(jnp.where(mask, hi.astype(F32), 0.0).astype(BF16))
            lows.append(jnp.where(mask, lo.astype(F32), 0.0).astype(BF16))
        spread = jnp.concatenate(highs + lows, axis=0)
        acc_ref[...] += dot_nt(spread, hot(lane, LANES))

    total = acc_ref[: 3 * keys] + acc_ref[3 * keys :]
    contact = jnp.concatenate(
        [
            jnp.concatenate([total[(c * wide + w) * nodes : (c * wide + w + 1) * nodes] for c in range(3)], axis=0)
            for w in range(wide)
        ],
        axis=1,
    )
    fold(state_ref[:half_rows] + 0.5 * contact, rows_ref)
    folded = fold_coef(coef_ref[...], 3)
    get, put = strided(rows_ref, folded.shape[0], nodes)
    run(solve_steps(get, put, hold_ref, folded, inv_ref, elim_ref, nodes))
    pos_ref[...] = unfold(rows_ref, half_rows)
    up, down = pack(pick(pos_ref[...], hot(cross_ref[pl.ds(step, 1), :], fdev)))
    rows = up.shape[0]
    up_ref[:rows] = up
    down_ref[:rows] = down
    up_ref[rows:] = rup_ref[...]
    down_ref[rows:] = rdown_ref[...]


def kept(cross_hot):
    ones = jnp.ones((8, cross_hot.shape[1]), BF16)
    return dot_nt(ones, cross_hot)[0:1] < 0.5


def arrive(up_ref, down_ref, values, cross_hot, keep, at):
    rows = pl.ds(at, values.shape[0] // 2)
    first, second = unpack(up_ref[rows, :], down_ref[rows, :])
    return jnp.where(keep, values, place(jnp.concatenate([first, second], axis=0), cross_hot))


def next_kernel(
    up_ref, down_ref, pos_ref, cross_ref, index_ref, fill_ref,
    state_ref, out_ref,
    table_ref, list_ref, *, step, nodes, fdev,
):
    cross_hot = hot(cross_ref[pl.ds(step - 1, 1), :], fdev)
    positions = arrive(up_ref, down_ref, pos_ref[...], cross_hot, kept(cross_hot), 0)
    state_ref[...] = positions
    store_table(table_ref, positions, nodes)
    send_gather(table_ref, index_ref.at[step], fill_ref, out_ref, list_ref, step, nodes, fdev)


def last_kernel(up_ref, down_ref, pos_ref, rot_ref, cross_ref, state_ref, *, step, nodes, fdev):
    rows = 3 * nodes
    cross_hot = hot(cross_ref[pl.ds(step, 1), :], fdev)
    keep = kept(cross_hot)
    state_ref[:rows] = arrive(up_ref, down_ref, pos_ref[...], cross_hot, keep, 0)
    state_ref[rows:] = arrive(up_ref, down_ref, rot_ref[...], cross_hot, keep, rows // 2)


def shifted(block, axis, distance):
    devices = range(lax.axis_size(axis))
    route = [((i - distance) % len(devices), i) for i in devices]
    return lax.ppermute(block, axis, route)


def per_device(state, stiffness, crossing, contact_send, contact_recv, contact_fill):
    fields, nodes, fdev = state.shape
    _, groups, quota = contact_send.shape
    blocks = quota // BLOCK
    pairs = groups * blocks
    cross = crossing.shape[1]
    rows = 3 * nodes
    moved = rows + 8
    lines = 3 * fdev // BLOCK
    vmem = pl.BlockSpec(memory_space=pltpu.VMEM)
    smem = pl.BlockSpec(memory_space=pltpu.SMEM)
    hbm = pl.BlockSpec(memory_space=pltpu.HBM)
    table = pltpu.VMEM((2 * rows * fdev // LANES, LANES), BF16)
    listed = pltpu.SMEM((pairs + 1,), jnp.int32)
    folded = pltpu.VMEM((lines * nodes, BLOCK), F32)

    def sds(*shape):
        return jax.ShapeDtypeStruct(shape, F32)

    sent_shape = sds(groups, 4 * blocks, BLOCK)
    factors = sds(nodes // 2, lines, BLOCK)

    hold = pltpu.VMEM((nodes, lines, BLOCK), F32)

    def call(kernel, name, ins, outs, scratch, flops, limit=VMEM_LIMIT, **static):
        return pl.pallas_call(
            functools.partial(kernel, nodes=nodes, fdev=fdev, **static),
            out_shape=outs,
            in_specs=ins,
            out_specs=[vmem] * len(outs),
            scratch_shapes=scratch,
            name=name,
            cost_estimate=pl.CostEstimate(flops=flops, bytes_accessed=4 * fields * nodes * fdev, transcendentals=0),
            compiler_params=pltpu.CompilerParams(vmem_limit_bytes=limit),
        )

    def by_block(index):
        return index.reshape(-1, groups, blocks, BLOCK).transpose(0, 2, 1, 3).reshape(-1, pairs, BLOCK)

    send, recv = by_block(contact_send), by_block(contact_recv)
    matmul = 2 * 2 * rows * fdev * groups * quota
    xcur = state.reshape(fields * nodes, fdev)
    coef = stiffness.reshape(1, fdev)
    (sent,) = call(
        first_kernel, "send_first", [hbm, hbm, smem], [sent_shape],
        [table, listed, pltpu.VMEM((rows, fdev), F32), pltpu.VMEM((pairs, BLOCK), jnp.int32),
         pltpu.SemaphoreType.DMA((2,))], matmul, limit=FIRST_LIMIT,
    )(xcur, send, contact_fill)
    got_shape = sds(groups, 3 * blocks, BLOCK)
    rot_moved = sds(rows // 2 + 8, cross)
    for step in range(STEPS):
        told = None if step == 0 else got
        got = lax.all_to_all(sent, "span", split_axis=0, concat_axis=0, tiled=True)
        if step == 0:
            local, inv, elim, rot, rup, rdown = call(
                local_kernel, "local", [vmem] * 4,
                [got_shape, factors, factors, sds(rows, fdev), rot_moved, rot_moved],
                [table, folded, hold], matmul,
            )(xcur, coef, crossing, recv)
        else:
            local, inv, elim, rot, coef, rup, rdown = call(
                local_next_kernel, "local_next", [vmem] * 8,
                [got_shape, factors, factors, sds(rows, fdev), sds(1, fdev), rot_moved, rot_moved],
                [table, listed], matmul, step=step,
            )(xcur, up, down, rot, coef, crossing, recv, told)
        pos, up, down = call(
            contact_kernel, "contact", [vmem] * 10,
            [sds(rows, fdev), sds(moved, cross), sds(moved, cross)],
            [pltpu.VMEM((2 * rows * fdev // LANES, LANES), F32), folded, hold,
             pltpu.VMEM((3, pairs + 8, BLOCK), F32), listed], matmul, step=step,
        )(got, local, recv, xcur, coef, inv, elim, crossing, rup, rdown)
        up = shifted(up, "stream", 1)
        down = shifted(down, "stream", -1)
        if step + 1 < STEPS:
            xcur, sent = call(
                next_kernel, "send_next", [vmem] * 5 + [smem],
                [sds(rows, fdev), sent_shape], [table, listed], matmul, step=step + 1,
            )(up, down, pos, crossing, send, contact_fill)
        else:
            (xcur,) = call(last_kernel, "arrive", [vmem] * 5, [sds(fields * nodes, fdev)], [], matmul // 8, step=step)(
                up, down, pos, rot, crossing
            )
    return xcur.reshape(fields, nodes, fdev)


def solution(mesh):
    placed = (
        P(None, None, ("span", "stream")),
        P(("span", "stream")),
        P(None, ("span", "stream")),
        P(None, None, ("span", "stream")),
        P(None, None, ("span", "stream")),
        P(None, None, ("span", "stream")),
    )
    return jax.shard_map(
        per_device,
        mesh=mesh,
        in_specs=placed,
        out_specs=P(None, None, ("span", "stream")),
        check_vma=False,
    )
```

time: 74 us -> 63.8 us (0.86)
  Pallas kernels: 37.9 us -> 27.3 us
  waiting for transfers between devices: 13.3 us -> 17.8 us
  local copies, waits for them, and re-layouts: 3.31 us -> 0.68 us
  starting transfers between devices: 18.9 us -> 17.8 us
    pallas_call x4, Pallas kernels: 24.5 us -> 18.4 us  [the longest x1 5.74 us: per_device(): call(first_kernel, 'send_first', [hbm, hbm, smem], [sent_shape], [table,...]
    pallas_call x2, Pallas kernels: 12 us -> 7.49 us  [per_device(): call(contact_kernel, 'contact', [vmem] * 10, [sds(rows, fdev), sds(moved,...]
    all_to_all x2, waiting for transfers between devices: 0.91 us -> 5.46 us  [per_device(): got = lax.all_to_all(sent, 'span', split_axis=0, concat_axis=0, tiled=True)]
    all_to_all x2, starting transfers between devices: 11 us -> 8.44 us  [per_device(): got = lax.all_to_all(sent, 'span', split_axis=0, concat_axis=0, tiled=True)]
    squeeze x3 -> x0, local copies, waits for them, and re-layouts: 1.49 us -> none  [the longest x1 0.78 us: per_device(): contact_send[step + 1]]
    ppermute x4, starting transfers between devices: 7.94 us -> 9.39 us  [shifted(): return lax.ppermute(block, axis, route)]
    unnamed x10 -> x12, local copies, waits for them, and re-layouts: 1.81 us -> 0.68 us
  transfers between devices with their start and end apart: 6 -> 6, of which waited for: 6 -> 6; matrix products, arithmetic and copies ran while one was open for 0% -> 0% of each run, Pallas kernels for 16% -> 12%
where the time goes in v1:
time: 63.8 us; the launch traced here: 63.7 us
  Pallas kernels  27.3 us (43%)
  starting transfers between devices  17.8 us (28%)
  waiting for transfers between devices  17.8 us (28%)
  local copies, waits for them, and re-layouts  0.68 us (1%)
    ppermute x4, waiting for transfers between devices, shifted(): return lax.ppermute(block, axis, route)  12.4 us
    ppermute x4, starting transfers between devices, shifted(): return lax.ppermute(block, axis, route)  9.39 us
    all_to_all x2, starting transfers between devices, per_device(): got = lax.all_to_all(sent, 'span', split_axis=0, concat_axis=0, tiled=True)  8.44 us
    pallas_call x2, Pallas kernels, per_device(): call(contact_kernel, 'contact', [vmem] * 10, [sds(rows, fdev), sds(moved,...  7.49 us
    pallas_call x1, Pallas kernels, per_device(): call(first_kernel, 'send_first', [hbm, hbm, smem], [sent_shape], [table,...  5.74 us
    all_to_all x2, waiting for transfers between devices, per_device(): got = lax.all_to_all(sent, 'span', split_axis=0, concat_axis=0, tiled=True)  5.46 us
    pallas_call x1, Pallas kernels, per_device(): call(next_kernel, 'send_next', [vmem] * 5 + [smem], [sds(rows, fdev), sen...  5.29 us
    pallas_call x1, Pallas kernels, per_device(): call(local_kernel, 'local', [vmem] * 4, [got_shape, factors, factors, sds...  4.2 us
  transfers between devices with their start and end apart: 6, of which 6 were waited for; matrix products, arithmetic and copies ran while one was open for 0% of the time, Pallas kernels for 12%

profile of v1, /device:TPU:105, one launch (start us, length us, event | category | flops | bytes accessed | tf_op | source)
XLA Modules:
  0.0 63.7 jit_solution(1667825322201219513)
XLA Ops:
  0.0 0.0 copy-start.1
  0.0 5.7 %send_first.1 = f32[8,32,128]{2,1,0:T(8,128)} custom-call(f32[384,512]{1,0:T(8,128)} %bitcast.13, s32[2,64,128]{2,1,0:T(8,128)} %bitcast.16, s32[2,8,8]{2,1,0:T(8,128)} %fill_ref.3), custom_call_target="tpu_custom_call" | custom-call | flops 3221225472 | bytes 786432 | tf_op jit(solution)/shard_map/send_first/pallas_call | solution.py:481
  5.7 0.0 copy-start.3
  5.8 4.7 %all-to-all-start = ((f32[8,32,128]{2,1,0:T(8,128)}), f32[8,32,128]{2,1,0:T(8,128)S(1)}, u32[]{:S(2)}, u32[]{:S(2)}) async-start(f32[8,32,128]{2,1,0:T(8,128)} %send_first.1), calls=%async_computation | async-start | bytes 262144 | tf_op jit(solution)/shard_map/all_to_all | solution.py:490
  10.5 0.0 copy-start.5
  10.5 0.0 copy-start
  10.5 0.0 copy-done.1
  10.5 0.0 copy-done.3
  10.5 0.6 %copy-done.5 = f32[512]{0:T(512)S(1)} copy-done((f32[512]{0:T(512)S(1)}, f32[512]{0:T(512)}, u32[]{:S(2)}) %copy-start.5) | copy-done | bytes 2072
  11.1 0.0 copy-done
  11.2 4.2 %local.1 = (f32[8,24,128]{2,1,0:T(8,128)S(1)}, f32[32,12,128]{2,1,0:T(8,128)S(1)}, f32[32,12,128]{2,1,0:T(8,128)S(1)}, f32[192,512]{1,0:T(8,128)S(1)}, f32[104,128]{1,0:T(8,128)S(1)}, /*index=5*/f32[104,128]{1,0:T(8,128)S(1)}) custom-call(f32[384,512]{1,0:T(8,128)S(1)} %bitcast.14, f32[1,512]{1,0:T(1,128)S(1)} %bitcast.22, s32[2,128]{1,0:T(2,128)S(1)} %copy-done, ...), custom_call_target="tpu_custom_call" | custom-call | flops 3221225472 | bytes 786432 | tf_op jit(solution)/shard_map/local/pallas_call | solution.py:492
  15.4 1.9 %all-to-all-done.got_ref.told_ref = f32[8,32,128]{2,1,0:T(8,128)S(1)} async-done(((f32[8,32,128]{2,1,0:T(8,128)}), f32[8,32,128]{2,1,0:T(8,128)S(1)}, u32[]{:S(2)}, u32[]{:S(2)}) %all-to-all-start) | async-done | bytes 131104 | tf_op jit(solution)/shard_map/all_to_all | solution.py:490
  17.3 0.0 copy-start.2
  17.3 0.0 copy-start.4
  17.3 3.8 %contact.2 = (f32[192,512]{1,0:T(8,128)S(1)}, f32[200,128]{1,0:T(8,128)S(1)}, f32[200,128]{1,0:T(8,128)S(1)}) custom-call(f32[8,32,128]{2,1,0:T(8,128)S(1)} %all-to-all-done.got_ref.told_ref, f32[8,24,128]{2,1,0:T(8,128)S(1)} %get-tuple-element.26.local_ref, s32[2,64,128]{2,1,0:T(8,128)S(1)} %bitcast.19, f32[384,512]{1,0:T(8,128)S(1)} %bitcast.15, ...), custom_call_target="tpu_custom_call" | custom-call | flops 3221225472 | bytes 786432 | tf_op jit(solution)/shard_map/contact/pallas_call | solution.py:503
  21.0 6.2 %collective-permute-start = (f32[200,128]{1,0:T(8,128)S(1)}, f32[200,128]{1,0:T(8,128)S(1)}, u32[]{:S(2)}, u32[]{:S(2)}) collective-permute-start(f32[200,128]{1,0:T(8,128)S(1)} %get-tuple-element.31), channel_id=1, source_target_pairs={{31,0},{0,1},{1,2},{2,3},{3,4},{4,5},{5,6},{6,7},{7,8},{8,9},{9,10... | collective-permute-start | bytes 307208 | tf_op jit(solution)/shard_map/ppermute | solution.py:435
  27.3 0.0 collective-permute-start.1
  27.3 1.7 %collective-permute-done.up_ref = f32[200,128]{1,0:T(8,128)S(1)} collective-permute-done((f32[200,128]{1,0:T(8,128)S(1)}, f32[200,128]{1,0:T(8,128)S(1)}, u32[]{:S(2)}, u32[]{:S(2)}) %collective-permute-start) | collective-permute-done | bytes 102432 | tf_op jit(solution)/shard_map/ppermute | solution.py:435
  28.9 4.5 %collective-permute-done.1.down_ref = f32[200,128]{1,0:T(8,128)S(1)} collective-permute-done((f32[200,128]{1,0:T(8,128)S(1)}, f32[200,128]{1,0:T(8,128)S(1)}, u32[]{:S(2)}, u32[]{:S(2)}) %collective-permute-start.1) | collective-permute-done | bytes 102432 | tf_op jit(solution)/shard_map/ppermute | solution.py:435
  33.5 0.0 copy-done.2
  33.5 0.0 copy-done.4
  33.5 5.3 %send_next.1 = (f32[192,512]{1,0:T(8,128)S(1)}, f32[8,32,128]{2,1,0:T(8,128)}) custom-call(f32[200,128]{1,0:T(8,128)S(1)} %collective-permute-done.up_ref, f32[200,128]{1,0:T(8,128)S(1)} %collective-permute-done.1.down_ref, f32[192,512]{1,0:T(8,128)S(1)} %get-tuple-element.33.pos_ref, s32[2,128]{1,0:T(2,128)S(1)} %copy-done, s32[2,64,128]{2,1,0:T(8,128)S(1)} %bitcast.17, ...), custom_call_target="tpu_custom_call" | custom-call | flops 3221225472 | bytes 786432 | tf_op jit(solution)/shard_map/send_next/pallas_call | solution.py:512
  38.8 3.7 %all-to-all-start.1 = ((f32[8,32,128]{2,1,0:T(8,128)}), f32[8,32,128]{2,1,0:T(8,128)S(1)}, u32[]{:S(2)}, u32[]{:S(2)}) async-start(f32[8,32,128]{2,1,0:T(8,128)} %get-tuple-element.34), calls=%async_computation.1 | async-start | bytes 262144 | tf_op jit(solution)/shard_map/all_to_all | solution.py:490
  42.5 3.2 %local_next.1 = (f32[8,24,128]{2,1,0:T(8,128)S(1)}, f32[32,12,128]{2,1,0:T(8,128)S(1)}, f32[32,12,128]{2,1,0:T(8,128)S(1)}, f32[192,512]{1,0:T(8,128)S(1)}, f32[...) custom-call(f32[192,512]{1,0:T(8,128)S(1)} %get-tuple-element.35.state_ref, ...), custom_call_target="tpu_custom_call" | custom-call | flops 3221225472 | bytes 786432 | tf_op jit(solution)/shard_map/local_next/pallas_call | solution.py:498
  45.7 3.6 %all-to-all-done.1.got_ref = f32[8,32,128]{2,1,0:T(8,128)S(1)} async-done(((f32[8,32,128]{2,1,0:T(8,128)}), f32[8,32,128]{2,1,0:T(8,128)S(1)}, u32[]{:S(2)}, u32[]{:S(2)}) %all-to-all-start.1) | async-done | bytes 131104 | tf_op jit(solution)/shard_map/all_to_all | solution.py:490
  49.3 3.7 %contact.3 = (f32[192,512]{1,0:T(8,128)S(1)}, f32[200,128]{1,0:T(8,128)S(1)}, f32[200,128]{1,0:T(8,128)S(1)}) custom-call(f32[8,32,128]{2,1,0:T(8,128)S(1)} %all-to-all-done.1.got_ref, f32[8,24,128]{2,1,0:T(8,128)S(1)} %get-tuple-element.37.local_ref, s32[2,64,128]{2,1,0:T(8,128)S(1)} %bitcast.21, f32[192,512]{1,0:T(8,128)S(1)} %get-tuple-element.35.state_ref, ...), custom_call_target="tpu_custom_call" | custom-call | flops 3221225472 | bytes 786432 | tf_op jit(solution)/shard_map/contact/pallas_call | solution.py:503
  53.0 3.1 %collective-permute-start.2 = (f32[200,128]{1,0:T(8,128)S(1)}, f32[200,128]{1,0:T(8,128)S(1)}, u32[]{:S(2)}, u32[]{:S(2)}) collective-permute-start(f32[200,128]{1,0:T(8,128)S(1)} %get-tuple-element.43), channel_id=1, source_target_pairs={{31,0},{0,1},{1,2},{2,3},{3,4},{4,5},{5,6},{6,7},{7,8},{8,9},{9,10... | collective-permute-start | bytes 307208 | tf_op jit(solution)/shard_map/ppermute | solution.py:435
  56.1 0.0 collective-permute-start.3
  56.1 1.7 %collective-permute-done.2.up_ref = f32[200,128]{1,0:T(8,128)S(1)} collective-permute-done((f32[200,128]{1,0:T(8,128)S(1)}, f32[200,128]{1,0:T(8,128)S(1)}, u32[]{:S(2)}, u32[]{:S(2)}) %collective-permute-start.2) | collective-permute-done | bytes 102432 | tf_op jit(solution)/shard_map/ppermute | solution.py:435
  57.8 4.5 %collective-permute-done.3.down_ref = f32[200,128]{1,0:T(8,128)S(1)} collective-permute-done((f32[200,128]{1,0:T(8,128)S(1)}, f32[200,128]{1,0:T(8,128)S(1)}, u32[]{:S(2)}, u32[]{:S(2)}) %collective-permute-start.3) | collective-permute-done | bytes 102432 | tf_op jit(solution)/shard_map/ppermute | solution.py:435
  62.3 1.4 %arrive.1 = f32[384,512]{1,0:T(8,128)} custom-call(f32[200,128]{1,0:T(8,128)S(1)} %collective-permute-done.2.up_ref, f32[200,128]{1,0:T(8,128)S(1)} %collective-permute-done.3.down_ref, f32[192,512]{1,0:T(8,128)S(1)} %get-tuple-element.45.pos_ref, f32[192,512]{1,0:T(8,128)S(1)} %get-tuple-element.46.rot_ref, s32[2,128]{1,0:T(2,128)S(1)} %copy-done), custom_call_target="tpu_custom_call" | custom-call | flops 402653184 | bytes 786432 | tf_op jit(solution)/shard_map/arrive/pallas_call | solution.py:517
Async XLA Ops:
  0.0 10.5 %copy-start.1 = (f32[6,64,512]{2,1,0:T(8,128)S(1)}, f32[6,64,512]{2,1,0:T(8,128)}, u32[]{:S(2)}) copy-start(f32[6,64,512]{2,1,0:T(8,128)} %param.6) | copy-start | bytes 2359300
  5.7 4.7 %copy-start.3 = (s32[2,8,1024]{2,1,0:T(8,128)S(1)}, s32[2,8,1024]{2,1,0:T(8,128)}, u32[]{:S(2)}) copy-start(s32[2,8,1024]{2,1,0:T(8,128)} %param.10) | copy-start | bytes 196612
  5.8 11.5 %all-to-all-start = ((f32[8,32,128]{2,1,0:T(8,128)}), f32[8,32,128]{2,1,0:T(8,128)S(1)}, u32[]{:S(2)}, u32[]{:S(2)}) async-start(f32[8,32,128]{2,1,0:T(8,128)} %send_first.1), calls=%async_computation | async-start | bytes 262144 | tf_op jit(solution)/shard_map/all_to_all | solution.py:490
  10.5 0.7 %copy-start.5 = (f32[512]{0:T(512)S(1)}, f32[512]{0:T(512)}, u32[]{:S(2)}) copy-start(f32[512]{0:T(512)} %param.7) | copy-start | bytes 6148
  10.5 0.7 %copy-start = (s32[2,128]{1,0:T(2,128)S(1)}, s32[2,128]{1,0:T(2,128)}, u32[]{:S(2)}) copy-start(s32[2,128]{1,0:T(2,128)} %cross_ref.11) | copy-start | bytes 3076
  17.3 16.2 %copy-start.2 = (s32[2,8,1024]{2,1,0:T(8,128)S(1)}, s32[2,8,1024]{2,1,0:T(8,128)}, u32[]{:S(2)}) copy-start(s32[2,8,1024]{2,1,0:T(8,128)} %param.9) | copy-start | bytes 196612
  17.3 16.2 %copy-start.4 = (s32[2,8,8]{2,1,0:T(8,128)S(1)}, s32[2,8,8]{2,1,0:T(8,128)}, u32[]{:S(2)}) copy-start(s32[2,8,8]{2,1,0:T(8,128)} %fill_ref.3) | copy-start | bytes 1540
  21.0 7.9 %collective-permute-start = (f32[200,128]{1,0:T(8,128)S(1)}, f32[200,128]{1,0:T(8,128)S(1)}, u32[]{:S(2)}, u32[]{:S(2)}) collective-permute-start(f32[200,128]{1,0:T(8,128)S(1)} %get-tuple-element.31), channel_id=1, source_target_pairs={{31,0},{0,1},{1,2},{2,3},{3,4},{4,5},{5,6},{6,7},{7,8},{8,9},{9,10... | collective-permute-start | bytes 307208 | tf_op jit(solution)/shard_map/ppermute | solution.py:435
  27.3 6.2 %collective-permute-start.1 = (f32[200,128]{1,0:T(8,128)S(1)}, f32[200,128]{1,0:T(8,128)S(1)}, u32[]{:S(2)}, u32[]{:S(2)}) collective-permute-start(f32[200,128]{1,0:T(8,128)S(1)} %get-tuple-element.32), channel_id=1, source_target_pairs={{1,0},{2,1},{3,2},{4,3},{5,4},{6,5},{7,6},{8,7},{9,8},{10,9},{11,1... | collective-permute-start | bytes 307208 | tf_op jit(solution)/shard_map/ppermute | solution.py:435
  38.8 10.5 %all-to-all-start.1 = ((f32[8,32,128]{2,1,0:T(8,128)}), f32[8,32,128]{2,1,0:T(8,128)S(1)}, u32[]{:S(2)}, u32[]{:S(2)}) async-start(f32[8,32,128]{2,1,0:T(8,128)} %get-tuple-element.34), calls=%async_computation.1 | async-start | bytes 262144 | tf_op jit(solution)/shard_map/all_to_all | solution.py:490
  53.0 4.8 %collective-permute-start.2 = (f32[200,128]{1,0:T(8,128)S(1)}, f32[200,128]{1,0:T(8,128)S(1)}, u32[]{:S(2)}, u32[]{:S(2)}) collective-permute-start(f32[200,128]{1,0:T(8,128)S(1)} %get-tuple-element.43), channel_id=1, source_target_pairs={{31,0},{0,1},{1,2},{2,3},{3,4},{4,5},{5,6},{6,7},{7,8},{8,9},{9,10... | collective-permute-start | bytes 307208 | tf_op jit(solution)/shard_map/ppermute | solution.py:435
  56.1 6.2 %collective-permute-start.3 = (f32[200,128]{1,0:T(8,128)S(1)}, f32[200,128]{1,0:T(8,128)S(1)}, u32[]{:S(2)}, u32[]{:S(2)}) collective-permute-start(f32[200,128]{1,0:T(8,128)S(1)} %get-tuple-element.44), channel_id=1, source_target_pairs={{1,0},{2,1},{3,2},{4,3},{5,4},{6,5},{7,6},{8,7},{9,8},{10,9},{11,1... | collective-permute-start | bytes 307208 | tf_op jit(solution)/shard_map/ppermute | solution.py:435

commit v2 on v1

--- a/solution.py
+++ b/solution.py
@@ -11,6 +11,7 @@
 BLOCK = 128
 LANES = 256
 CHUNK = 8
+PAD = 8
 F32 = jnp.float32
 BF16 = jnp.bfloat16
 VMEM_LIMIT = 48 * 1024 * 1024
@@ -64,15 +65,25 @@
 
 def gather_row(table, index, nodes, fdev, between=lambda: None):
     lane, per_node = parts_of(index, nodes)
-    key = row_key(per_node, nodes, fdev)
     got = jnp.dot(table, hot(lane, LANES), preferred_element_type=F32)
     between()
+    return select_rows(got, row_key(per_node, nodes, fdev))
+
+
+def arrived_row(table, slots, index, fdev):
+    slot = index & (fdev - 1)
+    onto = jnp.where(slots == slot, 1.0, 0.0).astype(BF16)
+    got = jnp.dot(table, onto, preferred_element_type=F32)
+    return select_rows(got, index >> (fdev.bit_length() - 1))
+
+
+def select_rows(got, key):
     rows = got.shape[0] // 2
     keys = rows // 3
-    relative = key - lax.broadcasted_iota(jnp.int32, (8, index.shape[1]), 0)
+    relative = key - lax.broadcasted_iota(jnp.int32, (8, key.shape[1]), 0)
     out = []
     for c in range(3):
-        acc = jnp.zeros((8, index.shape[1]), F32)
+        acc = jnp.zeros((8, key.shape[1]), F32)
         for j in range(0, keys, 8):
             at = c * keys + j
             acc = jnp.where(relative == j, got[at : at + 8] + got[rows + at : rows + at + 8], acc)
@@ -101,25 +112,58 @@
             out_ref[n >> (blocks.bit_length() - 1), pl.ds(at, 1), :] = rows[c][:, k * BLOCK : (k + 1) * BLOCK]
 
 
-def gather_live(table_ref, index_ref, out_ref, list_ref, count, groups, blocks, nodes, fdev):
-    @pl.loop(0, (count + CHUNK - 1) // CHUNK)
+def each_chunk(count, body):
+    chunks = (count + CHUNK - 1) // CHUNK
+    fours = chunks >> 2
+
+    @pl.loop(0, fours)
     def _(i):
-        ids = [list_ref[jnp.minimum(i * CHUNK + k, count - 1)] for k in range(CHUNK)]
-        index = index_chunk(index_ref, ids, groups, blocks)
-        put_chunk(out_ref, ids, gather_row(table_ref[...], index, nodes, fdev), blocks)
-
-
-def send_gather(table_ref, index_ref, fill_ref, out_ref, list_ref, step, nodes, fdev):
+        body([i * 4 + k for k in range(4)])
+
+    @pl.when((chunks & 2) > 0)
+    def _():
+        body([fours * 4, fours * 4 + 1])
+
+    @pl.when((chunks & 1) > 0)
+    def _():
+        body([chunks - 1])
+
+
+def gather_live(index_ref, out_ref, list_ref, count, groups, blocks, gather):
+    def body(numbers):
+        for i in numbers:
+            ids = [list_ref[jnp.minimum(i * CHUNK + k, count - 1)] for k in range(CHUNK)]
+            put_chunk(out_ref, ids, gather(index_chunk(index_ref, ids, groups, blocks)), blocks)
+
+    each_chunk(count, body)
+
+
+def get_chunk(ref, ids, blocks):
+    shift = blocks.bit_length() - 1
+    return [
+        jnp.concatenate([ref[n >> shift, pl.ds(c * blocks + (n & (blocks - 1)), 1), :] for n in ids], axis=1)
+        for c in range(3)
+    ]
+
+
+def send_start(fill_ref, out_ref, list_ref, step):
     groups, lines, _ = out_ref.shape
     blocks = lines // 4
     low = lax.broadcasted_iota(jnp.int32, (1, BLOCK), 1) < BLOCK // 2
     out_ref[...] = jnp.zeros_like(out_ref)
-    count = list_live(lambda g, b: (fill_ref[step, g, b] > 0).astype(jnp.int32), list_ref, groups, blocks)
     for g in range(groups):
         for b in range(blocks):
             fills = jnp.where(low, fill_ref[step, g, b], fill_ref[STEPS - 1, g, b])
             out_ref[g, pl.ds(3 * blocks + b, 1), :] = fills.astype(F32)
-    gather_live(table_ref, index_ref, out_ref, list_ref, count, groups, blocks, nodes, fdev)
+    return list_live(lambda g, b: (fill_ref[step, g, b] > 0).astype(jnp.int32), list_ref, groups, blocks)
+
+
+def send_gather(table_ref, index_ref, out_ref, list_ref, count, nodes, fdev):
+    groups, lines, _ = out_ref.shape
+    gather_live(
+        index_ref, out_ref, list_ref, count, groups, lines // 4,
+        lambda index: gather_row(table_ref[...], index, nodes, fdev),
+    )
 
 
 def live_words(got_ref, blocks, lane):
@@ -132,15 +176,23 @@
     return words
 
 
-def fold(values, rows_ref):
-    rows = values.shape[0]
+def fold(values, rows_ref, nodes):
+    fields = values.shape[0] // nodes
+    pitch = nodes + PAD
     for i in range(values.shape[1] // BLOCK):
-        rows_ref[i * rows : (i + 1) * rows] = values[:, i * BLOCK : (i + 1) * BLOCK]
-
-
-def unfold(rows_ref, rows):
-    chunks = rows_ref.shape[0] // rows
-    return jnp.concatenate([rows_ref[i * rows : (i + 1) * rows] for i in range(chunks)], axis=1)
+        for c in range(fields):
+            at = (i * fields + c) * pitch
+            rows_ref[at : at + nodes] = values[c * nodes : (c + 1) * nodes, i * BLOCK : (i + 1) * BLOCK]
+
+
+def unfold(rows_ref, rows, nodes):
+    fields = rows // nodes
+    pitch = nodes + PAD
+    lines = rows_ref.shape[0] // pitch
+    runs = [rows_ref[k * pitch : k * pitch + nodes] for k in range(lines)]
+    return jnp.concatenate(
+        [jnp.concatenate(runs[i : i + fields], axis=0) for i in range(0, lines, fields)], axis=1
+    )
 
 
 def fold_coef(coef, fields):
@@ -195,10 +247,10 @@
 
 def strided(rows_ref, lines, nodes):
     def get(n):
-        return rows_ref[pl.ds(n, lines, stride=nodes), :]
+        return rows_ref[pl.ds(n, lines, stride=nodes + PAD), :]
 
     def put(n, value):
-        rows_ref[pl.ds(n, lines, stride=nodes), :] = value
+        rows_ref[pl.ds(n, lines, stride=nodes + PAD), :] = value
 
     return get, put
 
@@ -252,16 +304,23 @@
 
 
 def first_kernel(
-    state_ref, index_ref, fill_ref, out_ref, table_ref, list_ref, held_ref, index_held_ref, sems, *, nodes, fdev
+    state_ref, index_ref, fill_ref, out_ref,
+    table_ref, list_ref, held_ref, index_held_ref, fill_held_ref, sems, *, nodes, fdev
 ):
-    copy = pltpu.make_async_copy(state_ref.at[pl.ds(0, 3 * nodes)], held_ref, sems.at[0])
-    index_copy = pltpu.make_async_copy(index_ref.at[0], index_held_ref, sems.at[1])
-    copy.start()
-    index_copy.start()
-    index_copy.wait()
-    copy.wait()
+    pairs = (
+        (fill_ref, fill_held_ref),
+        (state_ref.at[pl.ds(0, 3 * nodes)], held_ref),
+        (index_ref.at[0], index_held_ref),
+    )
+    copies = [pltpu.make_async_copy(src, dst, sems.at[i]) for i, (src, dst) in enumerate(pairs)]
+    for copy in copies:
+        copy.start()
+    copies[0].wait()
+    count = send_start(fill_held_ref, out_ref, list_ref, 0)
+    copies[1].wait()
     store_table(table_ref, held_ref[...], nodes)
-    send_gather(table_ref, index_held_ref, fill_ref, out_ref, list_ref, 0, nodes, fdev)
+    copies[2].wait()
+    send_gather(table_ref, index_held_ref, out_ref, list_ref, count, nodes, fdev)
 
 
 def local_kernel(
@@ -274,7 +333,7 @@
     blocks = lines // 3
     coef = coef_ref[...]
     folded = fold_coef(coef, 3)
-    fold(state_ref[half_rows:], rows_ref)
+    fold(state_ref[half_rows:], rows_ref, nodes)
     store_table(table_ref, state_ref[:half_rows], nodes)
 
     def chores():
@@ -295,7 +354,7 @@
         put_chunk(local_ref, ids, rows, blocks)
     run(steps)
 
-    rot_ref[...] = unfold(rows_ref, half_rows)
+    rot_ref[...] = unfold(rows_ref, half_rows, nodes)
     cross_hot = hot(cross_ref[pl.ds(0, 1), :], fdev)
     leave(rot_ref[...], coef, cross_hot, up_ref, down_ref)
 
@@ -311,8 +370,8 @@
 
 
 def local_next_kernel(
-    state_ref, up_ref, down_ref, rot_ref, coef_ref, cross_ref, index_ref, told_ref,
-    local_ref, inv_ref, elim_ref, rot_out_ref, coef_out_ref, rup_ref, rdown_ref,
+    up_ref, down_ref, pos_ref, rot_ref, coef_ref, cross_ref, index_ref, told_ref,
+    state_ref, local_ref, inv_ref, elim_ref, rot_out_ref, coef_out_ref, rup_ref, rdown_ref,
     table_ref, list_ref, *, step, nodes, fdev,
 ):
     groups, lines, _ = local_ref.shape
@@ -327,12 +386,17 @@
     first, _ = unpack(up_ref[rows, :], down_ref[rows, :])
     coef = jnp.where(keep, coef_ref[...], place(first, cross_hot)[0:1])
     coef_out_ref[...] = coef
-    store_table(table_ref, state_ref[...], nodes)
+    positions = arrive(up_ref, down_ref, pos_ref[...], cross_hot, keep, 0)
+    state_ref[...] = positions
+    store_table(table_ref, positions, nodes)
     run(factor_steps(fold_coef(coef, 3), inv_ref, elim_ref))
     rot = arrive(up_ref, down_ref, rot_ref[...], cross_hot, keep, part)
     rot_out_ref[...] = rot
     leave(rot, coef, hot(cross_ref[pl.ds(step, 1), :], fdev), rup_ref, rdown_ref)
-    gather_live(table_ref, index_ref.at[step], local_ref, list_ref, count, groups, blocks, nodes, fdev)
+    gather_live(
+        index_ref.at[step], local_ref, list_ref, count, groups, blocks,
+        lambda index: gather_row(table_ref[...], index, nodes, fdev),
+    )
 
 
 def contact_kernel(
@@ -361,8 +425,7 @@
     wide = fdev // LANES
     keys = wide * nodes
 
-    @pl.loop(0, (count + CHUNK - 1) // CHUNK)
-    def _(i):
+    def scattered(i):
         ids = [jnp.where(i * CHUNK + k < count, list_ref[i * CHUNK + k], pairs) for k in range(CHUNK)]
         index = index_chunk(index_ref.at[step], [jnp.minimum(n, pairs - 1) for n in ids], groups, blocks)
         lane, per_node = parts_of(index, nodes)
@@ -375,7 +438,15 @@
             highs.append(jnp.where(mask, hi.astype(F32), 0.0).astype(BF16))
             lows.append(jnp.where(mask, lo.astype(F32), 0.0).astype(BF16))
         spread = jnp.concatenate(highs + lows, axis=0)
-        acc_ref[...] += dot_nt(spread, hot(lane, LANES))
+        return dot_nt(spread, hot(lane, LANES))
+
+    def body(numbers):
+        total = scattered(numbers[0])
+        for i in numbers[1:]:
+            total = total + scattered(i)
+        acc_ref[...] += total
+
+    each_chunk(count, body)
 
     total = acc_ref[: 3 * keys] + acc_ref[3 * keys :]
     contact = jnp.concatenate(
@@ -385,11 +456,11 @@
         ],
         axis=1,
     )
-    fold(state_ref[:half_rows] + 0.5 * contact, rows_ref)
+    fold(state_ref[:half_rows] + 0.5 * contact, rows_ref, nodes)
     folded = fold_coef(coef_ref[...], 3)
     get, put = strided(rows_ref, folded.shape[0], nodes)
     run(solve_steps(get, put, hold_ref, folded, inv_ref, elim_ref, nodes))
-    pos_ref[...] = unfold(rows_ref, half_rows)
+    pos_ref[...] = unfold(rows_ref, half_rows, nodes)
     up, down = pack(pick(pos_ref[...], hot(cross_ref[pl.ds(step, 1), :], fdev)))
     rows = up.shape[0]
     up_ref[:rows] = up
@@ -409,24 +480,58 @@
     return jnp.where(keep, values, place(jnp.concatenate([first, second], axis=0), cross_hot))
 
 
+def own_kernel(
+    pos_ref, cross_ref, index_ref, fill_ref, out_ref, table_ref, list_ref, fill_held_ref, sem, *, step, nodes, fdev
+):
+    copy = pltpu.make_async_copy(fill_ref, fill_held_ref, sem)
+    copy.start()
+    keep = kept(hot(cross_ref[pl.ds(step - 1, 1), :], fdev))
+    store_table(table_ref, jnp.where(keep, pos_ref[...], 0.0), nodes)
+    copy.wait()
+    count = send_start(fill_held_ref, out_ref, list_ref, step)
+    send_gather(table_ref, index_ref.at[step], out_ref, list_ref, count, nodes, fdev)
+
+
 def next_kernel(
-    up_ref, down_ref, pos_ref, cross_ref, index_ref, fill_ref,
-    state_ref, out_ref,
-    table_ref, list_ref, *, step, nodes, fdev,
+    up_ref, down_ref, own_ref, cross_ref, index_ref, out_ref, table_ref, list_ref, *, step, nodes, fdev
 ):
-    cross_hot = hot(cross_ref[pl.ds(step - 1, 1), :], fdev)
-    positions = arrive(up_ref, down_ref, pos_ref[...], cross_hot, kept(cross_hot), 0)
-    state_ref[...] = positions
-    store_table(table_ref, positions, nodes)
-    send_gather(table_ref, index_ref.at[step], fill_ref, out_ref, list_ref, step, nodes, fdev)
-
-
-def last_kernel(up_ref, down_ref, pos_ref, rot_ref, cross_ref, state_ref, *, step, nodes, fdev):
+    groups, lines, _ = out_ref.shape
+    blocks = lines // 4
+    words = live_words(own_ref, blocks, 0)
+    count = list_live(lambda g, b: (words[g] >> b) & 1, list_ref, groups, blocks)
+    out_ref[...] = own_ref[...]
+    cross = cross_ref[pl.ds(step - 1, 1), :]
+    moved = cross.shape[1]
+    here = lax.broadcasted_iota(jnp.int32, (moved, moved), 0) == lax.broadcasted_iota(jnp.int32, (moved, moved), 1)
+    slots = jnp.sum(jnp.where(here, cross.astype(F32), 0.0), axis=1, keepdims=True).astype(jnp.int32)
+    part = 3 * nodes // 2
+    first, second = unpack(up_ref[:part, :], down_ref[:part, :])
+    hi, lo = split2(jnp.concatenate([first, second], axis=0))
+    table_ref[: 2 * part] = hi
+    table_ref[2 * part :] = lo
+
+    def body(numbers):
+        for i in numbers:
+            ids = [list_ref[jnp.minimum(i * CHUNK + k, count - 1)] for k in range(CHUNK)]
+            rows = arrived_row(table_ref[...], slots, index_chunk(index_ref.at[step], ids, groups, blocks), fdev)
+            held = get_chunk(own_ref, ids, blocks)
+            put_chunk(out_ref, ids, [a + b for a, b in zip(held, rows)], blocks)
+
+    each_chunk(count, body)
+
+
+def last_kernel(up_ref, down_ref, pos_ref, rot_ref, cross_ref, state_ref, done_ref, sems, *, step, nodes, fdev):
     rows = 3 * nodes
     cross_hot = hot(cross_ref[pl.ds(step, 1), :], fdev)
     keep = kept(cross_hot)
-    state_ref[:rows] = arrive(up_ref, down_ref, pos_ref[...], cross_hot, keep, 0)
-    state_ref[rows:] = arrive(up_ref, down_ref, rot_ref[...], cross_hot, keep, rows // 2)
+    copies = []
+    for i, ref in enumerate((pos_ref, rot_ref)):
+        side = pl.ds(i * rows, rows)
+        done_ref[side, :] = arrive(up_ref, down_ref, ref[...], cross_hot, keep, i * rows // 2)
+        copies.append(pltpu.make_async_copy(done_ref.at[side], state_ref.at[side], sems.at[i]))
+        copies[i].start()
+    for copy in copies:
+        copy.wait()
 
 
 def shifted(block, axis, distance):
@@ -445,11 +550,10 @@
     moved = rows + 8
     lines = 3 * fdev // BLOCK
     vmem = pl.BlockSpec(memory_space=pltpu.VMEM)
-    smem = pl.BlockSpec(memory_space=pltpu.SMEM)
     hbm = pl.BlockSpec(memory_space=pltpu.HBM)
     table = pltpu.VMEM((2 * rows * fdev // LANES, LANES), BF16)
     listed = pltpu.SMEM((pairs + 1,), jnp.int32)
-    folded = pltpu.VMEM((lines * nodes, BLOCK), F32)
+    folded = pltpu.VMEM((lines * (nodes + PAD), BLOCK), F32)
 
     def sds(*shape):
         return jax.ShapeDtypeStruct(shape, F32)
@@ -457,14 +561,15 @@
     sent_shape = sds(groups, 4 * blocks, BLOCK)
     factors = sds(nodes // 2, lines, BLOCK)
 
+    fills = pltpu.SMEM(contact_fill.shape, jnp.int32)
     hold = pltpu.VMEM((nodes, lines, BLOCK), F32)
 
-    def call(kernel, name, ins, outs, scratch, flops, limit=VMEM_LIMIT, **static):
+    def call(kernel, name, ins, outs, scratch, flops, limit=VMEM_LIMIT, space=vmem, **static):
         return pl.pallas_call(
             functools.partial(kernel, nodes=nodes, fdev=fdev, **static),
             out_shape=outs,
             in_specs=ins,
-            out_specs=[vmem] * len(outs),
+            out_specs=[space] * len(outs),
             scratch_shapes=scratch,
             name=name,
             cost_estimate=pl.CostEstimate(flops=flops, bytes_accessed=4 * fields * nodes * fdev, transcendentals=0),
@@ -479,9 +584,9 @@
     xcur = state.reshape(fields * nodes, fdev)
     coef = stiffness.reshape(1, fdev)
     (sent,) = call(
-        first_kernel, "send_first", [hbm, hbm, smem], [sent_shape],
+        first_kernel, "send_first", [hbm] * 3, [sent_shape],
         [table, listed, pltpu.VMEM((rows, fdev), F32), pltpu.VMEM((pairs, BLOCK), jnp.int32),
-         pltpu.SemaphoreType.DMA((2,))], matmul, limit=FIRST_LIMIT,
+         fills, pltpu.SemaphoreType.DMA((3,))], matmul, limit=FIRST_LIMIT,
     )(xcur, send, contact_fill)
     got_shape = sds(groups, 3 * blocks, BLOCK)
     rot_moved = sds(rows // 2 + 8, cross)
@@ -495,11 +600,11 @@
                 [table, folded, hold], matmul,
             )(xcur, coef, crossing, recv)
         else:
-            local, inv, elim, rot, coef, rup, rdown = call(
+            xcur, local, inv, elim, rot, coef, rup, rdown = call(
                 local_next_kernel, "local_next", [vmem] * 8,
-                [got_shape, factors, factors, sds(rows, fdev), sds(1, fdev), rot_moved, rot_moved],
+                [sds(rows, fdev), got_shape, factors, factors, sds(rows, fdev), sds(1, fdev), rot_moved, rot_moved],
                 [table, listed], matmul, step=step,
-            )(xcur, up, down, rot, coef, crossing, recv, told)
+            )(up, down, pos, rot, coef, crossing, recv, told)
         pos, up, down = call(
             contact_kernel, "contact", [vmem] * 10,
             [sds(rows, fdev), sds(moved, cross), sds(moved, cross)],
@@ -509,14 +614,20 @@
         up = shifted(up, "stream", 1)
         down = shifted(down, "stream", -1)
         if step + 1 < STEPS:
-            xcur, sent = call(
-                next_kernel, "send_next", [vmem] * 5 + [smem],
-                [sds(rows, fdev), sent_shape], [table, listed], matmul, step=step + 1,
-            )(up, down, pos, crossing, send, contact_fill)
+            (own,) = call(
+                own_kernel, "send_own", [vmem] * 4, [sent_shape],
+                [table, listed, fills, pltpu.SemaphoreType.DMA(())], matmul, step=step + 1,
+            )(pos, crossing, send, contact_fill)
+            (sent,) = call(
+                next_kernel, "send_next", [vmem] * 5, [sent_shape],
+                [pltpu.VMEM((2 * rows, cross), BF16), listed], matmul, step=step + 1,
+            )(up, down, own, crossing, send)
         else:
-            (xcur,) = call(last_kernel, "arrive", [vmem] * 5, [sds(fields * nodes, fdev)], [], matmul // 8, step=step)(
-                up, down, pos, rot, crossing
-            )
+            (xcur,) = call(
+                last_kernel, "arrive", [vmem] * 5, [sds(fields * nodes, fdev)],
+                [pltpu.VMEM((fields * nodes, fdev), F32), pltpu.SemaphoreType.DMA((2,))],
+                matmul // 8, space=hbm, step=step,
+            )(up, down, pos, rot, crossing)
     return xcur.reshape(fields, nodes, fdev)
 
 

time: 63.8 us -> 57.5 us (0.901)
  Pallas kernels: 27.3 us -> 24.7 us
  waiting for transfers between devices: 17.8 us -> 15.5 us
  starting transfers between devices: 17.8 us -> 15.9 us
    ppermute x4, waiting for transfers between devices: 12.4 us -> 9.91 us  [shifted(): return lax.ppermute(block, axis, route)]
    ppermute x4, starting transfers between devices: 9.39 us -> 7.03 us  [shifted(): return lax.ppermute(block, axis, route)]
    pallas_call x4 -> x5, Pallas kernels: 15.6 us -> 13.6 us  [the longest x1 4.68 us: per_device(): call(first_kernel, 'send_first', [hbm] * 3, [sent_shape], [table, listed,...]
  transfers between devices with their start and end apart: 6 -> 6, of which waited for: 6 -> 5; matrix products, arithmetic and copies ran while one was open for 0% -> 0% of each run, Pallas kernels for 12% -> 17%
where the time goes in v2:
time: 57.5 us; the launch traced here: 57 us
  Pallas kernels  24.7 us (43%)
  starting transfers between devices  15.9 us (28%)
  waiting for transfers between devices  15.5 us (27%)
  local copies, waits for them, and re-layouts  0.68 us (1%)
    ppermute x4, waiting for transfers between devices, shifted(): return lax.ppermute(block, axis, route)  9.91 us
    all_to_all x2, starting transfers between devices, per_device(): got = lax.all_to_all(sent, 'span', split_axis=0, concat_axis=0, tiled=True)  8.86 us
    pallas_call x2, Pallas kernels, per_device(): call(contact_kernel, 'contact', [vmem] * 10, [sds(rows, fdev), sds(moved,...  7.21 us
    ppermute x4, starting transfers between devices, shifted(): return lax.ppermute(block, axis, route)  7.03 us
    all_to_all x2, waiting for transfers between devices, per_device(): got = lax.all_to_all(sent, 'span', split_axis=0, concat_axis=0, tiled=True)  5.54 us
    pallas_call x1, Pallas kernels, per_device(): call(first_kernel, 'send_first', [hbm] * 3, [sent_shape], [table, listed,...  4.68 us
    pallas_call x1, Pallas kernels, per_device(): call(local_kernel, 'local', [vmem] * 4, [got_shape, factors, factors, sds...  3.86 us
    pallas_call x1, Pallas kernels, per_device(): call(local_next_kernel, 'local_next', [vmem] * 8, [sds(rows, fdev), got_s...  3.34 us
  transfers between devices with their start and end apart: 6, of which 5 were waited for; matrix products, arithmetic and copies ran while one was open for 0% of the time, Pallas kernels for 17%

profile of v2, /device:TPU:105, one launch (start us, length us, event | category | flops | bytes accessed | tf_op | source)
XLA Modules:
  0.0 57.0 jit_solution(9015088847845820809)
XLA Ops:
  0.0 0.0 copy-start.1
  0.0 4.7 %send_first.1 = f32[8,32,128]{2,1,0:T(8,128)} custom-call(f32[384,512]{1,0:T(8,128)} %bitcast.13, s32[2,64,128]{2,1,0:T(8,128)} %bitcast.16, s32[2,8,8]{2,1,0:T(8,128)} %fill_ref.3), custom_call_target="tpu_custom_call" | custom-call | flops 3221225472 | bytes 786432 | tf_op jit(solution)/shard_map/send_first/pallas_call | solution.py:586
  4.7 0.0 copy-start.3
  4.7 5.5 %all-to-all-start = ((f32[8,32,128]{2,1,0:T(8,128)}), f32[8,32,128]{2,1,0:T(8,128)S(1)}, u32[]{:S(2)}, u32[]{:S(2)}) async-start(f32[8,32,128]{2,1,0:T(8,128)} %send_first.1), calls=%async_computation | async-start | bytes 262144 | tf_op jit(solution)/shard_map/all_to_all | solution.py:595
  10.2 0.0 copy-start.5
  10.2 0.0 copy-start
  10.2 0.0 copy-done.1
  10.2 0.0 copy-done.3
  10.2 0.6 %copy-done.5 = f32[512]{0:T(512)S(1)} copy-done((f32[512]{0:T(512)S(1)}, f32[512]{0:T(512)}, u32[]{:S(2)}) %copy-start.5) | copy-done | bytes 2072
  10.9 0.0 copy-done
  10.9 3.9 %local.1 = (f32[8,24,128]{2,1,0:T(8,128)S(1)}, f32[32,12,128]{2,1,0:T(8,128)S(1)}, f32[32,12,128]{2,1,0:T(8,128)S(1)}, f32[192,512]{1,0:T(8,128)S(1)}, f32[104,128]{1,0:T(8,128)S(1)}, /*index=5*/f32[104,128]{1,0:T(8,128)S(1)}) custom-call(f32[384,512]{1,0:T(8,128)S(1)} %bitcast.14, f32[1,512]{1,0:T(1,128)S(1)} %bitcast.23, s32[2,128]{1,0:T(2,128)S(1)} %copy-done, ...), custom_call_target="tpu_custom_call" | custom-call | flops 3221225472 | bytes 786432 | tf_op jit(solution)/shard_map/local/pallas_call | solution.py:597
  14.8 2.2 %all-to-all-done.got_ref.told_ref = f32[8,32,128]{2,1,0:T(8,128)S(1)} async-done(((f32[8,32,128]{2,1,0:T(8,128)}), f32[8,32,128]{2,1,0:T(8,128)S(1)}, u32[]{:S(2)}, u32[]{:S(2)}) %all-to-all-start) | async-done | bytes 131104 | tf_op jit(solution)/shard_map/all_to_all | solution.py:595
  16.9 0.0 copy-start.2
  17.0 0.0 copy-start.4
  17.0 3.8 %contact.2 = (f32[192,512]{1,0:T(8,128)S(1)}, f32[200,128]{1,0:T(8,128)S(1)}, f32[200,128]{1,0:T(8,128)S(1)}) custom-call(f32[8,32,128]{2,1,0:T(8,128)S(1)} %all-to-all-done.got_ref.told_ref, f32[8,24,128]{2,1,0:T(8,128)S(1)} %get-tuple-element.25.local_ref, s32[2,64,128]{2,1,0:T(8,128)S(1)} %bitcast.20, f32[384,512]{1,0:T(8,128)S(1)} %bitcast.15, ...), custom_call_target="tpu_custom_call" | custom-call | flops 3221225472 | bytes 786432 | tf_op jit(solution)/shard_map/contact/pallas_call | solution.py:608
  20.8 5.0 %collective-permute-start = (f32[200,128]{1,0:T(8,128)S(1)}, f32[200,128]{1,0:T(8,128)S(1)}, u32[]{:S(2)}, u32[]{:S(2)}) collective-permute-start(f32[200,128]{1,0:T(8,128)S(1)} %get-tuple-element.30), channel_id=1, source_target_pairs={{31,0},{0,1},{1,2},{2,3},{3,4},{4,5},{5,6},{6,7},{7,8},{8,9},{9,10... | collective-permute-start | bytes 307208 | tf_op jit(solution)/shard_map/ppermute | solution.py:540
  25.8 0.0 collective-permute-start.1
  25.8 0.0 copy-done.2
  25.8 0.0 copy-done.4
  25.8 2.5 %send_own.1.own_ref = f32[8,32,128]{2,1,0:T(8,128)S(1)} custom-call(f32[192,512]{1,0:T(8,128)S(1)} %get-tuple-element.32.pos_ref, s32[2,128]{1,0:T(2,128)S(1)} %copy-done, s32[2,64,128]{2,1,0:T(8,128)S(1)} %bitcast.17, s32[2,8,8]{2,1,0:T(8,128)S(1)} %copy-done.4), custom_call_target="tpu_custom_call" | custom-call | flops 3221225472 | bytes 786432 | tf_op jit(solution)/shard_map/send_own/pallas_call | solution.py:617
  28.3 0.0 collective-permute-done.up_ref
  28.3 3.7 %collective-permute-done.1.down_ref = f32[200,128]{1,0:T(8,128)S(1)} collective-permute-done((f32[200,128]{1,0:T(8,128)S(1)}, f32[200,128]{1,0:T(8,128)S(1)}, u32[]{:S(2)}, u32[]{:S(2)}) %collective-permute-start.1) | collective-permute-done | bytes 102432 | tf_op jit(solution)/shard_map/ppermute | solution.py:540
  32.0 1.9 %send_next.1 = f32[8,32,128]{2,1,0:T(8,128)} custom-call(f32[200,128]{1,0:T(8,128)S(1)} %collective-permute-done.up_ref, f32[200,128]{1,0:T(8,128)S(1)} %collective-permute-done.1.down_ref, f32[8,32,128]{2,1,0:T(8,128)S(1)} %send_own.1.own_ref, s32[2,128]{1,0:T(2,128)S(1)} %copy-done, s32[2,64,128]{2,1,0:T(8,128)S(1)} %bitcast.18), custom_call_target="tpu_custom_call" | custom-call | flops 3221225472 | bytes 786432 | tf_op jit(solution)/shard_map/send_next/pallas_call | solution.py:621
  33.9 3.4 %all-to-all-start.1 = ((f32[8,32,128]{2,1,0:T(8,128)}), f32[8,32,128]{2,1,0:T(8,128)S(1)}, u32[]{:S(2)}, u32[]{:S(2)}) async-start(f32[8,32,128]{2,1,0:T(8,128)} %send_next.1), calls=%async_computation.1 | async-start | bytes 262144 | tf_op jit(solution)/shard_map/all_to_all | solution.py:595
  37.3 3.3 %local_next.1 = (f32[192,512]{1,0:T(8,128)S(1)}, f32[8,24,128]{2,1,0:T(8,128)S(1)}, f32[32,12,128]{2,1,0:T(8,128)S(1)}, f32[32,12,128]{2,1,0:T(8,128)S(1)}, f32[...) custom-call(f32[200,128]{1,0:T(8,128)S(1)} %collective-permute-done.up_ref, ...), custom_call_target="tpu_custom_call" | custom-call | flops 3221225472 | bytes 786432 | tf_op jit(solution)/shard_map/local_next/pallas_call | solution.py:603
  40.6 3.3 %all-to-all-done.1.got_ref = f32[8,32,128]{2,1,0:T(8,128)S(1)} async-done(((f32[8,32,128]{2,1,0:T(8,128)}), f32[8,32,128]{2,1,0:T(8,128)S(1)}, u32[]{:S(2)}, u32[]{:S(2)}) %all-to-all-start.1) | async-done | bytes 131104 | tf_op jit(solution)/shard_map/all_to_all | solution.py:595
  43.9 3.4 %contact.3 = (f32[192,512]{1,0:T(8,128)S(1)}, f32[200,128]{1,0:T(8,128)S(1)}, f32[200,128]{1,0:T(8,128)S(1)}) custom-call(f32[8,32,128]{2,1,0:T(8,128)S(1)} %all-to-all-done.1.got_ref, f32[8,24,128]{2,1,0:T(8,128)S(1)} %get-tuple-element.34.local_ref, s32[2,64,128]{2,1,0:T(8,128)S(1)} %bitcast.22, f32[192,512]{1,0:T(8,128)S(1)} %get-tuple-element.35.state_ref, ...), custom_call_target="tpu_custom_call" | custom-call | flops 3221225472 | bytes 786432 | tf_op jit(solution)/shard_map/contact/pallas_call | solution.py:608
  47.3 2.0 %collective-permute-start.2 = (f32[200,128]{1,0:T(8,128)S(1)}, f32[200,128]{1,0:T(8,128)S(1)}, u32[]{:S(2)}, u32[]{:S(2)}) collective-permute-start(f32[200,128]{1,0:T(8,128)S(1)} %get-tuple-element.41), channel_id=1, source_target_pairs={{31,0},{0,1},{1,2},{2,3},{3,4},{4,5},{5,6},{6,7},{7,8},{8,9},{9,10... | collective-permute-start | bytes 307208 | tf_op jit(solution)/shard_map/ppermute | solution.py:540
  49.3 0.0 collective-permute-start.3
  49.3 1.7 %collective-permute-done.2.up_ref = f32[200,128]{1,0:T(8,128)S(1)} collective-permute-done((f32[200,128]{1,0:T(8,128)S(1)}, f32[200,128]{1,0:T(8,128)S(1)}, u32[]{:S(2)}, u32[]{:S(2)}) %collective-permute-start.2) | collective-permute-done | bytes 102432 | tf_op jit(solution)/shard_map/ppermute | solution.py:540
  51.0 4.5 %collective-permute-done.3.down_ref = f32[200,128]{1,0:T(8,128)S(1)} collective-permute-done((f32[200,128]{1,0:T(8,128)S(1)}, f32[200,128]{1,0:T(8,128)S(1)}, u32[]{:S(2)}, u32[]{:S(2)}) %collective-permute-start.3) | collective-permute-done | bytes 102432 | tf_op jit(solution)/shard_map/ppermute | solution.py:540
  55.5 1.3 %arrive.1 = f32[384,512]{1,0:T(8,128)} custom-call(f32[200,128]{1,0:T(8,128)S(1)} %collective-permute-done.2.up_ref, f32[200,128]{1,0:T(8,128)S(1)} %collective-permute-done.3.down_ref, f32[192,512]{1,0:T(8,128)S(1)} %get-tuple-element.43.pos_ref, f32[192,512]{1,0:T(8,128)S(1)} %get-tuple-element.44.rot_ref, s32[2,128]{1,0:T(2,128)S(1)} %copy-done), custom_call_target="tpu_custom_call" | custom-call | flops 402653184 | bytes 786432 | tf_op jit(solution)/shard_map/arrive/pallas_call | solution.py:626
Async XLA Ops:
  0.0 10.2 %copy-start.1 = (f32[6,64,512]{2,1,0:T(8,128)S(1)}, f32[6,64,512]{2,1,0:T(8,128)}, u32[]{:S(2)}) copy-start(f32[6,64,512]{2,1,0:T(8,128)} %param.6) | copy-start | bytes 2359300
  4.7 5.5 %copy-start.3 = (s32[2,8,1024]{2,1,0:T(8,128)S(1)}, s32[2,8,1024]{2,1,0:T(8,128)}, u32[]{:S(2)}) copy-start(s32[2,8,1024]{2,1,0:T(8,128)} %param.10) | copy-start | bytes 196612
  4.7 12.3 %all-to-all-start = ((f32[8,32,128]{2,1,0:T(8,128)}), f32[8,32,128]{2,1,0:T(8,128)S(1)}, u32[]{:S(2)}, u32[]{:S(2)}) async-start(f32[8,32,128]{2,1,0:T(8,128)} %send_first.1), calls=%async_computation | async-start | bytes 262144 | tf_op jit(solution)/shard_map/all_to_all | solution.py:595
  10.2 0.7 %copy-start.5 = (f32[512]{0:T(512)S(1)}, f32[512]{0:T(512)}, u32[]{:S(2)}) copy-start(f32[512]{0:T(512)} %param.7) | copy-start | bytes 6148
  10.2 0.7 %copy-start = (s32[2,128]{1,0:T(2,128)S(1)}, s32[2,128]{1,0:T(2,128)}, u32[]{:S(2)}) copy-start(s32[2,128]{1,0:T(2,128)} %cross_ref.13) | copy-start | bytes 3076
  16.9 8.9 %copy-start.2 = (s32[2,8,1024]{2,1,0:T(8,128)S(1)}, s32[2,8,1024]{2,1,0:T(8,128)}, u32[]{:S(2)}) copy-start(s32[2,8,1024]{2,1,0:T(8,128)} %param.9) | copy-start | bytes 196612
  17.0 8.9 %copy-start.4 = (s32[2,8,8]{2,1,0:T(8,128)S(1)}, s32[2,8,8]{2,1,0:T(8,128)}, u32[]{:S(2)}) copy-start(s32[2,8,8]{2,1,0:T(8,128)} %fill_ref.3) | copy-start | bytes 1540
  20.8 7.5 %collective-permute-start = (f32[200,128]{1,0:T(8,128)S(1)}, f32[200,128]{1,0:T(8,128)S(1)}, u32[]{:S(2)}, u32[]{:S(2)}) collective-permute-start(f32[200,128]{1,0:T(8,128)S(1)} %get-tuple-element.30), channel_id=1, source_target_pairs={{31,0},{0,1},{1,2},{2,3},{3,4},{4,5},{5,6},{6,7},{7,8},{8,9},{9,10... | collective-permute-start | bytes 307208 | tf_op jit(solution)/shard_map/ppermute | solution.py:540
  25.8 6.2 %collective-permute-start.1 = (f32[200,128]{1,0:T(8,128)S(1)}, f32[200,128]{1,0:T(8,128)S(1)}, u32[]{:S(2)}, u32[]{:S(2)}) collective-permute-start(f32[200,128]{1,0:T(8,128)S(1)} %get-tuple-element.31), channel_id=1, source_target_pairs={{1,0},{2,1},{3,2},{4,3},{5,4},{6,5},{7,6},{8,7},{9,8},{10,9},{11,1... | collective-permute-start | bytes 307208 | tf_op jit(solution)/shard_map/ppermute | solution.py:540
  33.9 10.1 %all-to-all-start.1 = ((f32[8,32,128]{2,1,0:T(8,128)}), f32[8,32,128]{2,1,0:T(8,128)S(1)}, u32[]{:S(2)}, u32[]{:S(2)}) async-start(f32[8,32,128]{2,1,0:T(8,128)} %send_next.1), calls=%async_computation.1 | async-start | bytes 262144 | tf_op jit(solution)/shard_map/all_to_all | solution.py:595
  47.3 3.7 %collective-permute-start.2 = (f32[200,128]{1,0:T(8,128)S(1)}, f32[200,128]{1,0:T(8,128)S(1)}, u32[]{:S(2)}, u32[]{:S(2)}) collective-permute-start(f32[200,128]{1,0:T(8,128)S(1)} %get-tuple-element.41), channel_id=1, source_target_pairs={{31,0},{0,1},{1,2},{2,3},{3,4},{4,5},{5,6},{6,7},{7,8},{8,9},{9,10... | collective-permute-start | bytes 307208 | tf_op jit(solution)/shard_map/ppermute | solution.py:540
  49.3 6.2 %collective-permute-start.3 = (f32[200,128]{1,0:T(8,128)S(1)}, f32[200,128]{1,0:T(8,128)S(1)}, u32[]{:S(2)}, u32[]{:S(2)}) collective-permute-start(f32[200,128]{1,0:T(8,128)S(1)} %get-tuple-element.42), channel_id=1, source_target_pairs={{1,0},{2,1},{3,2},{4,3},{5,4},{6,5},{7,6},{8,7},{9,8},{10,9},{11,1... | collective-permute-start | bytes 307208 | tf_op jit(solution)/shard_map/ppermute | solution.py:540

commit v3 on v2

--- a/solution.py
+++ b/solution.py
@@ -131,9 +131,8 @@
 
 def gather_live(index_ref, out_ref, list_ref, count, groups, blocks, gather):
     def body(numbers):
-        for i in numbers:
-            ids = [list_ref[jnp.minimum(i * CHUNK + k, count - 1)] for k in range(CHUNK)]
-            put_chunk(out_ref, ids, gather(index_chunk(index_ref, ids, groups, blocks)), blocks)
+        ids = [list_ref[jnp.minimum(i * CHUNK + k, count - 1)] for i in numbers for k in range(CHUNK)]
+        put_chunk(out_ref, ids, gather(index_chunk(index_ref, ids, groups, blocks)), blocks)
 
     each_chunk(count, body)
 
@@ -425,8 +424,9 @@
     wide = fdev // LANES
     keys = wide * nodes
 
-    def scattered(i):
-        ids = [jnp.where(i * CHUNK + k < count, list_ref[i * CHUNK + k], pairs) for k in range(CHUNK)]
+    def body(numbers):
+        places = [i * CHUNK + k for i in numbers for k in range(CHUNK)]
+        ids = [jnp.where(n < count, list_ref[n], pairs) for n in places]
         index = index_chunk(index_ref.at[step], [jnp.minimum(n, pairs - 1) for n in ids], groups, blocks)
         lane, per_node = parts_of(index, nodes)
         key = row_key(per_node, nodes, fdev)
@@ -438,13 +438,7 @@
             highs.append(jnp.where(mask, hi.astype(F32), 0.0).astype(BF16))
             lows.append(jnp.where(mask, lo.astype(F32), 0.0).astype(BF16))
         spread = jnp.concatenate(highs + lows, axis=0)
-        return dot_nt(spread, hot(lane, LANES))
-
-    def body(numbers):
-        total = scattered(numbers[0])
-        for i in numbers[1:]:
-            total = total + scattered(i)
-        acc_ref[...] += total
+        acc_ref[...] += dot_nt(spread, hot(lane, LANES))
 
     each_chunk(count, body)
 

time: 57.5 us -> 58.1 us (1.010)
  starting transfers between devices: 15.9 us -> 17.3 us
  waiting for transfers between devices: 15.5 us -> 14.3 us
    ppermute x4, waiting for transfers between devices: 9.91 us -> 8.7 us  [shifted(): return lax.ppermute(block, axis, route)]
    pallas_call x1, Pallas kernels: 2.45 us -> 3.66 us  [per_device(): call(own_kernel, 'send_own', [vmem] * 4, [sent_shape], [table, listed, fi...]
    ppermute x4, starting transfers between devices: 7.03 us -> 8.08 us  [shifted(): return lax.ppermute(block, axis, route)]
    pallas_call x2, Pallas kernels: 7.21 us -> 6.17 us  [per_device(): call(contact_kernel, 'contact', [vmem] * 10, [sds(rows, fdev), sds(moved,...]
    pallas_call x1, Pallas kernels: 4.68 us -> 3.67 us  [per_device(): call(first_kernel, 'send_first', [hbm] * 3, [sent_shape], [table, listed,...]
    pallas_call x1, Pallas kernels: 1.86 us -> 2.48 us  [per_device(): call(next_kernel, 'send_next', [vmem] * 5, [sent_shape], [pltpu.VMEM((2 *...]
  transfers between devices with their start and end apart: 6 -> 6, of which waited for: 5 -> 5; matrix products, arithmetic and copies ran while one was open for 0% -> 0% of each run, Pallas kernels for 17% -> 19%
where the time goes in v3:
time: 58.1 us; the launch traced here: 57 us
  Pallas kernels  24.4 us (42%)
  starting transfers between devices  17.3 us (30%)
  waiting for transfers between devices  14.3 us (25%)
  local copies, waits for them, and re-layouts  0.68 us (1%)
    all_to_all x2, starting transfers between devices, per_device(): got = lax.all_to_all(sent, 'span', split_axis=0, concat_axis=0, tiled=True)  9.27 us
    ppermute x4, waiting for transfers between devices, shifted(): return lax.ppermute(block, axis, route)  8.7 us
    ppermute x4, starting transfers between devices, shifted(): return lax.ppermute(block, axis, route)  8.08 us
    pallas_call x2, Pallas kernels, per_device(): call(contact_kernel, 'contact', [vmem] * 10, [sds(rows, fdev), sds(moved,...  6.17 us
    all_to_all x2, waiting for transfers between devices, per_device(): got = lax.all_to_all(sent, 'span', split_axis=0, concat_axis=0, tiled=True)  5.57 us
    pallas_call x1, Pallas kernels, per_device(): call(local_kernel, 'local', [vmem] * 4, [got_shape, factors, factors, sds...  3.86 us
    pallas_call x1, Pallas kernels, per_device(): call(first_kernel, 'send_first', [hbm] * 3, [sent_shape], [table, listed,...  3.67 us
    pallas_call x1, Pallas kernels, per_device(): call(own_kernel, 'send_own', [vmem] * 4, [sent_shape], [table, listed, fi...  3.66 us
  transfers between devices with their start and end apart: 6, of which 5 were waited for; matrix products, arithmetic and copies ran while one was open for 0% of the time, Pallas kernels for 19%

profile of v3, /device:TPU:105, one launch (start us, length us, event | category | flops | bytes accessed | tf_op | source)
XLA Modules:
  0.0 57.0 jit_solution(17990586798694885263)
XLA Ops:
  0.0 0.0 copy-start.1
  0.0 3.7 %send_first.1 = f32[8,32,128]{2,1,0:T(8,128)} custom-call(f32[384,512]{1,0:T(8,128)} %bitcast.13, s32[2,64,128]{2,1,0:T(8,128)} %bitcast.16, s32[2,8,8]{2,1,0:T(8,128)} %fill_ref.3), custom_call_target="tpu_custom_call" | custom-call | flops 3221225472 | bytes 786432 | tf_op jit(solution)/shard_map/send_first/pallas_call | solution.py:580
  3.7 0.0 copy-start.3
  3.7 5.9 %all-to-all-start = ((f32[8,32,128]{2,1,0:T(8,128)}), f32[8,32,128]{2,1,0:T(8,128)S(1)}, u32[]{:S(2)}, u32[]{:S(2)}) async-start(f32[8,32,128]{2,1,0:T(8,128)} %send_first.1), calls=%async_computation | async-start | bytes 262144 | tf_op jit(solution)/shard_map/all_to_all | solution.py:589
  9.6 0.0 copy-start.5
  9.6 0.0 copy-start
  9.6 0.0 copy-done.1
  9.6 0.0 copy-done.3
  9.6 0.6 %copy-done.5 = f32[512]{0:T(512)S(1)} copy-done((f32[512]{0:T(512)S(1)}, f32[512]{0:T(512)}, u32[]{:S(2)}) %copy-start.5) | copy-done | bytes 2072
  10.3 0.0 copy-done
  10.3 3.9 %local.1 = (f32[8,24,128]{2,1,0:T(8,128)S(1)}, f32[32,12,128]{2,1,0:T(8,128)S(1)}, f32[32,12,128]{2,1,0:T(8,128)S(1)}, f32[192,512]{1,0:T(8,128)S(1)}, f32[104,128]{1,0:T(8,128)S(1)}, /*index=5*/f32[104,128]{1,0:T(8,128)S(1)}) custom-call(f32[384,512]{1,0:T(8,128)S(1)} %bitcast.14, f32[1,512]{1,0:T(1,128)S(1)} %bitcast.23, s32[2,128]{1,0:T(2,128)S(1)} %copy-done, ...), custom_call_target="tpu_custom_call" | custom-call | flops 3221225472 | bytes 786432 | tf_op jit(solution)/shard_map/local/pallas_call | solution.py:591
  14.2 2.2 %all-to-all-done.got_ref.told_ref = f32[8,32,128]{2,1,0:T(8,128)S(1)} async-done(((f32[8,32,128]{2,1,0:T(8,128)}), f32[8,32,128]{2,1,0:T(8,128)S(1)}, u32[]{:S(2)}, u32[]{:S(2)}) %all-to-all-start) | async-done | bytes 131104 | tf_op jit(solution)/shard_map/all_to_all | solution.py:589
  16.4 0.0 copy-start.2
  16.4 0.0 copy-start.4
  16.4 2.8 %contact.2 = (f32[192,512]{1,0:T(8,128)S(1)}, f32[200,128]{1,0:T(8,128)S(1)}, f32[200,128]{1,0:T(8,128)S(1)}) custom-call(f32[8,32,128]{2,1,0:T(8,128)S(1)} %all-to-all-done.got_ref.told_ref, f32[8,24,128]{2,1,0:T(8,128)S(1)} %get-tuple-element.25.local_ref, s32[2,64,128]{2,1,0:T(8,128)S(1)} %bitcast.20, f32[384,512]{1,0:T(8,128)S(1)} %bitcast.15, ...), custom_call_target="tpu_custom_call" | custom-call | flops 3221225472 | bytes 786432 | tf_op jit(solution)/shard_map/contact/pallas_call | solution.py:602
  19.1 6.9 %collective-permute-start = (f32[200,128]{1,0:T(8,128)S(1)}, f32[200,128]{1,0:T(8,128)S(1)}, u32[]{:S(2)}, u32[]{:S(2)}) collective-permute-start(f32[200,128]{1,0:T(8,128)S(1)} %get-tuple-element.30), channel_id=1, source_target_pairs={{31,0},{0,1},{1,2},{2,3},{3,4},{4,5},{5,6},{6,7},{7,8},{8,9},{9,10... | collective-permute-start | bytes 307208 | tf_op jit(solution)/shard_map/ppermute | solution.py:534
  26.1 0.0 collective-permute-start.1
  26.1 0.0 copy-done.2
  26.1 0.0 copy-done.4
  26.1 3.7 %send_own.1.own_ref = f32[8,32,128]{2,1,0:T(8,128)S(1)} custom-call(f32[192,512]{1,0:T(8,128)S(1)} %get-tuple-element.32.pos_ref, s32[2,128]{1,0:T(2,128)S(1)} %copy-done, s32[2,64,128]{2,1,0:T(8,128)S(1)} %bitcast.17, s32[2,8,8]{2,1,0:T(8,128)S(1)} %copy-done.4), custom_call_target="tpu_custom_call" | custom-call | flops 3221225472 | bytes 786432 | tf_op jit(solution)/shard_map/send_own/pallas_call | solution.py:611
  29.7 0.0 collective-permute-done.up_ref
  29.8 2.5 %collective-permute-done.1.down_ref = f32[200,128]{1,0:T(8,128)S(1)} collective-permute-done((f32[200,128]{1,0:T(8,128)S(1)}, f32[200,128]{1,0:T(8,128)S(1)}, u32[]{:S(2)}, u32[]{:S(2)}) %collective-permute-start.1) | collective-permute-done | bytes 102432 | tf_op jit(solution)/shard_map/ppermute | solution.py:534
  32.3 2.5 %send_next.1 = f32[8,32,128]{2,1,0:T(8,128)} custom-call(f32[200,128]{1,0:T(8,128)S(1)} %collective-permute-done.up_ref, f32[200,128]{1,0:T(8,128)S(1)} %collective-permute-done.1.down_ref, f32[8,32,128]{2,1,0:T(8,128)S(1)} %send_own.1.own_ref, s32[2,128]{1,0:T(2,128)S(1)} %copy-done, s32[2,64,128]{2,1,0:T(8,128)S(1)} %bitcast.18), custom_call_target="tpu_custom_call" | custom-call | flops 3221225472 | bytes 786432 | tf_op jit(solution)/shard_map/send_next/pallas_call | solution.py:615
  34.7 3.4 %all-to-all-start.1 = ((f32[8,32,128]{2,1,0:T(8,128)}), f32[8,32,128]{2,1,0:T(8,128)S(1)}, u32[]{:S(2)}, u32[]{:S(2)}) async-start(f32[8,32,128]{2,1,0:T(8,128)} %send_next.1), calls=%async_computation.1 | async-start | bytes 262144 | tf_op jit(solution)/shard_map/all_to_all | solution.py:589
  38.1 3.3 %local_next.1 = (f32[192,512]{1,0:T(8,128)S(1)}, f32[8,24,128]{2,1,0:T(8,128)S(1)}, f32[32,12,128]{2,1,0:T(8,128)S(1)}, f32[32,12,128]{2,1,0:T(8,128)S(1)}, f32[...) custom-call(f32[200,128]{1,0:T(8,128)S(1)} %collective-permute-done.up_ref, ...), custom_call_target="tpu_custom_call" | custom-call | flops 3221225472 | bytes 786432 | tf_op jit(solution)/shard_map/local_next/pallas_call | solution.py:597
  41.4 3.4 %all-to-all-done.1.got_ref = f32[8,32,128]{2,1,0:T(8,128)S(1)} async-done(((f32[8,32,128]{2,1,0:T(8,128)}), f32[8,32,128]{2,1,0:T(8,128)S(1)}, u32[]{:S(2)}, u32[]{:S(2)}) %all-to-all-start.1) | async-done | bytes 131104 | tf_op jit(solution)/shard_map/all_to_all | solution.py:589
  44.8 3.4 %contact.3 = (f32[192,512]{1,0:T(8,128)S(1)}, f32[200,128]{1,0:T(8,128)S(1)}, f32[200,128]{1,0:T(8,128)S(1)}) custom-call(f32[8,32,128]{2,1,0:T(8,128)S(1)} %all-to-all-done.1.got_ref, f32[8,24,128]{2,1,0:T(8,128)S(1)} %get-tuple-element.34.local_ref, s32[2,64,128]{2,1,0:T(8,128)S(1)} %bitcast.22, f32[192,512]{1,0:T(8,128)S(1)} %get-tuple-element.35.state_ref, ...), custom_call_target="tpu_custom_call" | custom-call | flops 3221225472 | bytes 786432 | tf_op jit(solution)/shard_map/contact/pallas_call | solution.py:602
  48.2 1.2 %collective-permute-start.2 = (f32[200,128]{1,0:T(8,128)S(1)}, f32[200,128]{1,0:T(8,128)S(1)}, u32[]{:S(2)}, u32[]{:S(2)}) collective-permute-start(f32[200,128]{1,0:T(8,128)S(1)} %get-tuple-element.41), channel_id=1, source_target_pairs={{31,0},{0,1},{1,2},{2,3},{3,4},{4,5},{5,6},{6,7},{7,8},{8,9},{9,10... | collective-permute-start | bytes 307208 | tf_op jit(solution)/shard_map/ppermute | solution.py:534
  49.4 0.0 collective-permute-start.3
  49.4 1.7 %collective-permute-done.2.up_ref = f32[200,128]{1,0:T(8,128)S(1)} collective-permute-done((f32[200,128]{1,0:T(8,128)S(1)}, f32[200,128]{1,0:T(8,128)S(1)}, u32[]{:S(2)}, u32[]{:S(2)}) %collective-permute-start.2) | collective-permute-done | bytes 102432 | tf_op jit(solution)/shard_map/ppermute | solution.py:534
  51.0 4.5 %collective-permute-done.3.down_ref = f32[200,128]{1,0:T(8,128)S(1)} collective-permute-done((f32[200,128]{1,0:T(8,128)S(1)}, f32[200,128]{1,0:T(8,128)S(1)}, u32[]{:S(2)}, u32[]{:S(2)}) %collective-permute-start.3) | collective-permute-done | bytes 102432 | tf_op jit(solution)/shard_map/ppermute | solution.py:534
  55.6 1.3 %arrive.1 = f32[384,512]{1,0:T(8,128)} custom-call(f32[200,128]{1,0:T(8,128)S(1)} %collective-permute-done.2.up_ref, f32[200,128]{1,0:T(8,128)S(1)} %collective-permute-done.3.down_ref, f32[192,512]{1,0:T(8,128)S(1)} %get-tuple-element.43.pos_ref, f32[192,512]{1,0:T(8,128)S(1)} %get-tuple-element.44.rot_ref, s32[2,128]{1,0:T(2,128)S(1)} %copy-done), custom_call_target="tpu_custom_call" | custom-call | flops 402653184 | bytes 786432 | tf_op jit(solution)/shard_map/arrive/pallas_call | solution.py:620
Async XLA Ops:
  0.0 9.6 %copy-start.1 = (f32[6,64,512]{2,1,0:T(8,128)S(1)}, f32[6,64,512]{2,1,0:T(8,128)}, u32[]{:S(2)}) copy-start(f32[6,64,512]{2,1,0:T(8,128)} %param.6) | copy-start | bytes 2359300
  3.7 5.9 %copy-start.3 = (s32[2,8,1024]{2,1,0:T(8,128)S(1)}, s32[2,8,1024]{2,1,0:T(8,128)}, u32[]{:S(2)}) copy-start(s32[2,8,1024]{2,1,0:T(8,128)} %param.10) | copy-start | bytes 196612
  3.7 12.7 %all-to-all-start = ((f32[8,32,128]{2,1,0:T(8,128)}), f32[8,32,128]{2,1,0:T(8,128)S(1)}, u32[]{:S(2)}, u32[]{:S(2)}) async-start(f32[8,32,128]{2,1,0:T(8,128)} %send_first.1), calls=%async_computation | async-start | bytes 262144 | tf_op jit(solution)/shard_map/all_to_all | solution.py:589
  9.6 0.7 %copy-start.5 = (f32[512]{0:T(512)S(1)}, f32[512]{0:T(512)}, u32[]{:S(2)}) copy-start(f32[512]{0:T(512)} %param.7) | copy-start | bytes 6148
  9.6 0.7 %copy-start = (s32[2,128]{1,0:T(2,128)S(1)}, s32[2,128]{1,0:T(2,128)}, u32[]{:S(2)}) copy-start(s32[2,128]{1,0:T(2,128)} %cross_ref.13) | copy-start | bytes 3076
  16.4 9.7 %copy-start.2 = (s32[2,8,1024]{2,1,0:T(8,128)S(1)}, s32[2,8,1024]{2,1,0:T(8,128)}, u32[]{:S(2)}) copy-start(s32[2,8,1024]{2,1,0:T(8,128)} %param.9) | copy-start | bytes 196612
  16.4 9.7 %copy-start.4 = (s32[2,8,8]{2,1,0:T(8,128)S(1)}, s32[2,8,8]{2,1,0:T(8,128)}, u32[]{:S(2)}) copy-start(s32[2,8,8]{2,1,0:T(8,128)} %fill_ref.3) | copy-start | bytes 1540
  19.1 10.6 %collective-permute-start = (f32[200,128]{1,0:T(8,128)S(1)}, f32[200,128]{1,0:T(8,128)S(1)}, u32[]{:S(2)}, u32[]{:S(2)}) collective-permute-start(f32[200,128]{1,0:T(8,128)S(1)} %get-tuple-element.30), channel_id=1, source_target_pairs={{31,0},{0,1},{1,2},{2,3},{3,4},{4,5},{5,6},{6,7},{7,8},{8,9},{9,10... | collective-permute-start | bytes 307208 | tf_op jit(solution)/shard_map/ppermute | solution.py:534
  26.1 6.2 %collective-permute-start.1 = (f32[200,128]{1,0:T(8,128)S(1)}, f32[200,128]{1,0:T(8,128)S(1)}, u32[]{:S(2)}, u32[]{:S(2)}) collective-permute-start(f32[200,128]{1,0:T(8,128)S(1)} %get-tuple-element.31), channel_id=1, source_target_pairs={{1,0},{2,1},{3,2},{4,3},{5,4},{6,5},{7,6},{8,7},{9,8},{10,9},{11,1... | collective-permute-start | bytes 307208 | tf_op jit(solution)/shard_map/ppermute | solution.py:534
  34.7 10.1 %all-to-all-start.1 = ((f32[8,32,128]{2,1,0:T(8,128)}), f32[8,32,128]{2,1,0:T(8,128)S(1)}, u32[]{:S(2)}, u32[]{:S(2)}) async-start(f32[8,32,128]{2,1,0:T(8,128)} %send_next.1), calls=%async_computation.1 | async-start | bytes 262144 | tf_op jit(solution)/shard_map/all_to_all | solution.py:589
  48.2 2.8 %collective-permute-start.2 = (f32[200,128]{1,0:T(8,128)S(1)}, f32[200,128]{1,0:T(8,128)S(1)}, u32[]{:S(2)}, u32[]{:S(2)}) collective-permute-start(f32[200,128]{1,0:T(8,128)S(1)} %get-tuple-element.41), channel_id=1, source_target_pairs={{31,0},{0,1},{1,2},{2,3},{3,4},{4,5},{5,6},{6,7},{7,8},{8,9},{9,10... | collective-permute-start | bytes 307208 | tf_op jit(solution)/shard_map/ppermute | solution.py:534
  49.4 6.2 %collective-permute-start.3 = (f32[200,128]{1,0:T(8,128)S(1)}, f32[200,128]{1,0:T(8,128)S(1)}, u32[]{:S(2)}, u32[]{:S(2)}) collective-permute-start(f32[200,128]{1,0:T(8,128)S(1)} %get-tuple-element.42), channel_id=1, source_target_pairs={{1,0},{2,1},{3,2},{4,3},{5,4},{6,5},{7,6},{8,7},{9,8},{10,9},{11,1... | collective-permute-start | bytes 307208 | tf_op jit(solution)/shard_map/ppermute | solution.py:534
